TPU v7x, 256 devices: a whole 4x4x8 slice. The times are simulated.
256 devices in a mesh: dp: 8 (over x_lo, y), owner: 8 (over z), context: 4 (over x_hi, core).
Axes of the slice: x: 4 (x_hi: 2, x_lo: 2; x = x_hi * 2 + x_lo), y: 4, z: 8, core: 2. Of those that a mesh axis runs over, the one named last changes fastest.
Arguments:
- grad_partials: bfloat16 [32, 1536, 64, 192], P(('dp', 'context'), None, 'owner')
- assignment: int32 [64, 1], replicated, may hold values from 0 to 7; in each aligned block of 8 rows (0 to 7, 8 to 15, ...) at most 2 rows name the same one
- momentum: float32 [128, 1536, 192], P('owner', ('dp', 'context')), may hold values from -6 to 6
- q_weight: float32 [128, 1536, 192], P('owner', ('dp', 'context')), may hold values from -1.2 to 1.2
- k_weight: float32 [64, 512, 128], P('owner', ('dp', 'context')), may hold values from -6 to 6
- max_logits: float32 [4, 64], P('context'), may hold values from 20 to 400
Outputs:
- momentum_out: float32 [128, 1536, 192], P('owner', ('dp', 'context'))
- q_weight_out: float32 [128, 1536, 192], P('owner', ('dp', 'context'))
- k_weight_out: float32 [64, 512, 128], P('owner', ('dp', 'context'))
Inputs may be any that keep to these rules, and one draw needn't show every extreme that they name: `assignment`: in each aligned block of 8 heads no owner index is named more than 2 times, and some owner index exactly 2 times.
All inputs are finite; a program needn't handle non-finite values.
Results may differ from a plain program's by a relative error of at most 0.0007.
Values may be sent and summed in bfloat16 or wider, within the bound.
A program may use at most 128 MiB of HBM per device.

v0:
```python
import math

import jax
import jax.numpy as jnp
from jax import lax
from jax.sharding import PartitionSpec as P

QR = 1536
QK = 192
ITERS = 2


MOMENTUM_RATE = 0.95
WEIGHT_KEEP = 0.98
LOGIT_CAP = 100.0
QUINTIC_A = 3.4445
QUINTIC_B = -4.775
QUINTIC_C = 2.0315


def routing(assignment, heads_own, per_source):
    target = assignment[:, 0]
    head_index = jnp.arange(target.shape[0], dtype=jnp.int32)
    source_block = head_index // heads_own
    earlier = (
        (source_block[None, :] == source_block[:, None])
        & (head_index[None, :] < head_index[:, None])
        & (target[None, :] == target[:, None])
    )
    position = jnp.sum(earlier.astype(jnp.int32), axis=1)
    return (target, position, source_block * per_source + position)


def refresh(weight, orthogonal, gamma, kn_count):
    step_size = 0.04 * math.sqrt(max(QR, QK))
    column_index = jnp.arange(weight.shape[2])
    column_scale = jnp.where(
        column_index[None, :] < kn_count, jnp.sqrt(gamma)[:, None], gamma[:, None]
    )
    return (WEIGHT_KEEP * weight - step_size * orthogonal.astype(jnp.float32)) * column_scale[
        :, None, :
    ]


def quintic(whole):
    for step in range(ITERS):
        gram_matrix = jnp.einsum("nrk,nrl->nkl", whole, whole, preferred_element_type=jnp.float32)
        polynomial = (
            QUINTIC_B * gram_matrix
            + QUINTIC_C
            * jnp.einsum("nkl,nlm->nkm", gram_matrix, gram_matrix, precision=lax.Precision.HIGHEST)
        ).astype(jnp.bfloat16)
        whole = (
            QUINTIC_A * whole.astype(jnp.float32)
            + jnp.einsum("nrk,nkl->nrl", whole, polynomial, preferred_element_type=jnp.float32)
        ).astype(jnp.bfloat16)
    return whole


def orthogonalize(matrix):
    square_sum = lax.psum(jnp.sum(matrix * matrix, axis=(1, 2)), ("dp", "context"))
    iterate = (matrix / (jnp.sqrt(square_sum) + 1e-07)[:, None, None]).astype(jnp.bfloat16)
    row_count = matrix.shape[1]
    gathered = lax.all_gather(iterate, ("dp", "context"), axis=1, tiled=True)
    gathered = quintic(gathered)
    return lax.dynamic_slice_in_dim(
        gathered, lax.axis_index(("dp", "context")) * row_count, row_count, 1
    )


def body(grad_partials, assignment, momentum, q_weight, k_weight, max_logits):
    heads_own = grad_partials.shape[2]
    slots_own = momentum.shape[0]
    kn_count = k_weight.shape[2]
    per_source = slots_own // lax.axis_size("owner")
    my_owner = lax.axis_index("owner")
    target, position, local_slot = routing(assignment, heads_own, per_source)
    peak_logit = lax.pmax(max_logits[0], "context")
    gamma = jnp.minimum(1.0, LOGIT_CAP / peak_logit)
    partial_value = grad_partials[0]
    grad_rows = lax.psum_scatter(
        partial_value.astype(jnp.float32), ("dp", "context"), scatter_dimension=0, tiled=True
    )
    home_target = lax.dynamic_slice_in_dim(target, my_owner * heads_own, heads_own)
    home_position = lax.dynamic_slice_in_dim(position, my_owner * heads_own, heads_own)
    send_index = home_target * per_source + home_position
    slot_index = jnp.arange(slots_own, dtype=jnp.int32)
    sender = (slot_index[:, None] == send_index[None, :]).astype(jnp.float32)
    owned_mask = (
        (target[None, :] == my_owner) & (local_slot[None, :] == slot_index[:, None])
    ).astype(jnp.float32)
    occupied = (jnp.sum(owned_mask, axis=1) > 0.5)[:, None, None]
    home_gamma = lax.dynamic_slice_in_dim(gamma, my_owner * heads_own, heads_own)
    outgoing = jnp.einsum("qi,rik->qrk", sender, grad_rows, precision=lax.Precision.HIGHEST)
    arrived = lax.all_to_all(outgoing, "owner", split_axis=0, concat_axis=0, tiled=True)
    refreshed = jnp.where(occupied, MOMENTUM_RATE * momentum + arrived, momentum)
    orthogonal = orthogonalize(refreshed)
    slot_gamma = jnp.sum(owned_mask * gamma[None, :], axis=1)
    slot_gamma = jnp.where(occupied[:, 0, 0], slot_gamma, 1.0)
    q_weight_out = jnp.where(
        occupied, refresh(q_weight, orthogonal, slot_gamma, kn_count), q_weight
    )
    k_weight_out = k_weight * jnp.sqrt(home_gamma)[:, None, None]
    return (refreshed, q_weight_out, k_weight_out)


def solution(mesh):
    placed = (
        P(("dp", "context"), None, "owner", None),
        P(),
        P("owner", ("dp", "context"), None),
        P("owner", ("dp", "context"), None),
        P("owner", ("dp", "context"), None),
        P("context", None),
    )
    return jax.shard_map(
        body,
        mesh=mesh,
        in_specs=placed,
        out_specs=(
            P("owner", ("dp", "context"), None),
            P("owner", ("dp", "context"), None),
            P("owner", ("dp", "context"), None),
        ),
        check_vma=False,
    )
```

profile of v0, /device:TPU:1, one launch (start us, length us, event | category | flops | bytes accessed | tf_op | source)
XLA Modules:
  0.0 456.4 jit_solution(1013946448971146130)
XLA Ops:
  7.2 0.0 reduce-scatter.2.cloned.1.call-start
  7.2 9.2 %copy.57 = bf16[1,1536,8,192]{3,2,1,0:T(8,128)(2,1)} copy(bf16[1,1536,8,192]{1,3,2,0:T(8,128)(2,1)} %param.6) | data formatting | bytes 9437184 | tf_op args[0]
  16.4 7.5 %bitcast_convert_fusion = f32[1536,8,192]{2,1,0:T(8,128)} fusion(bf16[1,1536,8,192]{3,2,1,0:T(8,128)(2,1)} %copy.57), kind=kLoop, calls=%fused_computation.4 | loop fusion | flops 2359296 | bytes 14155776 | tf_op jit(solution)/shard_map/convert_element_type | solution.py:82
  23.8 0.0 reduce-scatter.2.cloned.1.call-update
  23.9 0.6 copy-done.4
  24.5 0.2 convert_reduce_fusion
  24.7 0.1 fusion.13
  24.7 175.2 %reduce-scatter.2.cloned.1.call-done = f32[48,8,192]{2,1,0:T(8,128)} async-done(((f32[1536,8,192]{2,1,0:T(8,128)}), f32[48,8,192]{2,1,0:T(8,128)}) %reduce-scatter.2.cloned.1.call-update) | async-done | bytes 294928 | tf_op jit(solution)/shard_map/reduce_scatter | solution.py:81
  199.9 1.6 fusion.8
  201.5 1.3 copy.58
  202.9 8.6 %all-to-all-start = ((f32[16,48,192]{2,1,0:T(8,128)}), f32[16,48,192]{2,1,0:T(8,128)S(1)}, u32[]{:S(2)}, u32[]{:S(2)}) async-start(f32[16,48,192]{2,1,0:T(8,128)} %copy.58), calls=%async_computation.1 | async-start | bytes 1572864 | tf_op jit(solution)/shard_map/all_to_all | solution.py:95
  211.5 0.0 all-gather.2.cloned.1.call-start
  211.5 10.9 %pmax.7 = f32[64]{0:T(128)S(1)} all-reduce(f32[64]{0:T(128)S(1)} %bitcast.24), channel_id=1, replica_groups=mesh['dp'=8,'owner'=8,'context'=4] {'context'}, use_global_device_ids=true, to_apply=%region_5.6 | all-reduce | flops 64 | bytes 512 | tf_op jit(solution)/shard_map/pmax | solution.py:78
  222.4 0.1 select_reduce_fusion
  222.5 8.9 %all-to-all-done = f32[16,48,192]{2,1,0:T(8,128)S(1)} async-done(((f32[16,48,192]{2,1,0:T(8,128)}), f32[16,48,192]{2,1,0:T(8,128)S(1)}, u32[]{:S(2)}, u32[]{:S(2)}) %all-to-all-start) | async-done | bytes 589856 | tf_op jit(solution)/shard_map/all_to_all | solution.py:95
  231.4 0.3 multiply_reduce_fusion
  231.8 66.2 %psum.7 = f32[16]{0:T(128)S(1)} all-reduce(f32[16]{0:T(128)S(1)} %get-tuple-element.16), channel_id=1, replica_groups=mesh['dp'=8,'owner'=8,'context'=4] {'dp','context'}, use_global_device_ids=true, to_apply=%region_4.5 | all-reduce | flops 16 | bytes 128 | tf_op jit(solution)/shard_map/psum | solution.py:61
  297.9 0.1 divide_convert_fusion
  298.1 0.9 copy.59
  298.9 0.0 all-gather.2.cloned.1.call-update
  299.0 0.1 dynamic-slice_sqrt_fusion
  299.1 0.1 broadcast_select_fusion
  299.1 0.7 broadcast_multiply_fusion
  299.9 73.1 %all-gather.2.cloned.1.call-done = bf16[16,1536,192]{2,0,1:T(8,128)(2,1)} async-done(((bf16[16,48,192]{2,0,1:T(8,128)(2,1)}), bf16[16,1536,192]{2,0,1:T(8,128)(2,1)}) %all-gather.2.cloned.1.call-update) | async-done | bytes 9437200 | tf_op jit(solution)/shard_map/all_gather | solution.py:64
  373.0 21.7 %fusion = f32[16,192,192]{2,1,0:T(8,128)S(1)} fusion(bf16[16,1536,192]{2,0,1:T(8,128)(2,1)} %all-gather.2.cloned.1.call-done), kind=kOutput, calls=%fused_computation.1 | convolution fusion | flops 1811939328 | bytes 11796480 | tf_op jit(solution)/shard_map/nrk,nrl->nkl/dot_general | solution.py:47
  394.7 3.6 add_convert_fusion.2
  398.3 17.7 %add_convert_fusion = bf16[16,1536,192]{2,1,0:T(8,128)(2,1)} fusion(bf16[16,192,192]{2,1,0:T(8,128)(2,1)S(1)} %add_convert_fusion.2, bf16[16,1536,192]{2,0,1:T(8,128)(2,1)} %all-gather.2.cloned.1.call-done), kind=kOutput, calls=%fused_computation | convolution fusion | flops 1830813696 | bytes 20054016 | tf_op jit(solution)/shard_map/nrk,nkl->nrl/dot_general | solution.py:55
  416.0 11.3 %fusion.15 = f32[16,192,192]{2,1,0:T(8,128)S(1)} fusion(bf16[16,1536,192]{2,1,0:T(8,128)(2,1)} %add_convert_fusion), kind=kOutput, calls=%fused_computation.44 | convolution fusion | flops 1811939328 | bytes 11796480 | tf_op jit(solution)/shard_map/nrk,nrl->nkl/dot_general | solution.py:47
  427.4 3.5 add_convert_fusion.1
  430.8 0.0 copy-start.2
  430.9 16.4 %fusion.16 = f32[16,1536,192]{2,1,0:T(8,128)} fusion(bf16[16,1536,192]{2,1,0:T(8,128)(2,1)} %add_convert_fusion, bf16[16,192,192]{2,1,0:T(8,128)(2,1)S(1)} %add_convert_fusion.1), kind=kOutput, calls=%fused_computation.45 | convolution fusion | flops 1811939328 | bytes 29491200 | tf_op jit(solution)/shard_map/nrk,nkl->nrl/dot_general | solution.py:55
  447.2 2.4 multiply_select_fusion
  (18 shorter events, 0.1 us)
Async XLA Ops:
  7.2 192.8 %reduce-scatter.2.cloned.1.call-start = ((), (), s32[]{:S(2)}) async-start(), calls=%async_computation.2 | async-start | bytes 12976128 | tf_op jit(solution)/shard_map/reduce_scatter | solution.py:81
  23.8 0.7 copy-start.4
  23.9 187.7 %copy-start.5 = (f32[1,64]{1,0:T(1,128)S(1)}, f32[1,64]{1,0:T(1,128)}, u32[]{:S(2)}) copy-start(f32[1,64]{1,0:T(1,128)} %param.11) | copy-start | bytes 772
  23.9 207.6 %copy-start.1 = (f32[16,48,192]{2,1,0:T(8,128)S(1)}, f32[16,48,192]{2,1,0:T(8,128)}, u32[]{:S(2)}) copy-start(f32[16,48,192]{2,1,0:T(8,128)} %param.8) | copy-start | bytes 1769476
  202.9 96.3 %copy-start.3 = (f32[8,16,128]{2,1,0:T(8,128)S(1)}, f32[8,16,128]{2,1,0:T(8,128)}, u32[]{:S(2)}) copy-start(f32[8,16,128]{2,1,0:T(8,128)} %param.10) | copy-start | bytes 196612
  202.9 28.6 %all-to-all-start = ((f32[16,48,192]{2,1,0:T(8,128)}), f32[16,48,192]{2,1,0:T(8,128)S(1)}, u32[]{:S(2)}, u32[]{:S(2)}) async-start(f32[16,48,192]{2,1,0:T(8,128)} %copy.58), calls=%async_computation.1 | async-start | bytes 1572864 | tf_op jit(solution)/shard_map/all_to_all | solution.py:95
  211.5 161.5 %all-gather.2.cloned.1.call-start = ((), (), s32[]{:S(2)}) async-start(), calls=%async_computation.3 | async-start | bytes 12976128 | tf_op jit(solution)/shard_map/all_gather | solution.py:64
  231.7 163.0 %copy-start = (f32[16,48,192]{2,1,0:T(8,128)}, f32[16,48,192]{2,1,0:T(8,128)S(1)}, u32[]{:S(2)}) copy-start(f32[16,48,192]{2,1,0:T(8,128)S(1)} %get-tuple-element.17) | copy-start | bytes 1769476
  430.8 16.4 %copy-start.2 = (f32[16,48,192]{2,1,0:T(8,128)S(1)}, f32[16,48,192]{2,1,0:T(8,128)}, u32[]{:S(2)}) copy-start(f32[16,48,192]{2,1,0:T(8,128)} %param.9) | copy-start | bytes 1769476
Sparse Core Ops, SparseCore 0:
  24.0 175.8 reduce-scatter.1
  299.1 73.8 all-gather.1
where the time goes:
time: 457 us; the launch traced here: 456 us
  waiting for transfers between devices  257 us (56%)
  blocking collectives  77 us (17%)
  matrix products  75.8 us (17%)
  between operations  14.2 us (3%)
  local copies, waits for them, and re-layouts  12.1 us (3%)
  other arithmetic  11.5 us (3%)
  starting transfers between devices  8.69 us (2%)
    reduce_scatter x1, waiting for transfers between devices, body(): lax.psum_scatter(partial_value.astype(jnp.float32), ('dp', 'context'), sc...  175 us
    all_gather x1, waiting for transfers between devices, orthogonalize(): gathered = lax.all_gather(iterate, ('dp', 'context'), axis=1, tiled=True)  73.1 us
    psum x1, blocking collectives, orthogonalize(): lax.psum(jnp.sum(matrix * matrix, axis=(1, 2)), ('dp', 'context'))  66.2 us
    dot_general x2, matrix products, quintic(): jnp.einsum('nrk,nkl->nrl', whole, polynomial, preferred_element_type=jnp....  34.1 us
    dot_general x2, matrix products, quintic(): jnp.einsum('nrk,nrl->nkl', whole, whole, preferred_element_type=jnp.float32)  33.1 us
    pmax x1, blocking collectives, body(): peak_logit = lax.pmax(max_logits[0], 'context')  10.9 us
    unnamed x13, local copies, waits for them, and re-layouts  9.79 us
  transfers between devices with their start and end apart: 3, of which 3 were waited for; matrix products, arithmetic and copies ran while one was open for 0% of the time, Pallas kernels for 0%

commit v1 on v0

v1 whole, which is shorter than its diff:
```python
import functools
import math

import jax
import jax.numpy as jnp
from jax import lax
from jax.experimental import pallas as pl
from jax.experimental.pallas import tpu as pltpu
from jax.sharding import PartitionSpec as P

QR = 1536
QK = 192
ITERS = 2
MOMENTUM_RATE = 0.95
WEIGHT_KEEP = 0.98
LOGIT_CAP = 100.0
QUINTIC_A = 3.4445
QUINTIC_B = -4.775
QUINTIC_C = 2.0315

MESH = pl.DeviceIdType.MESH
BLOCKS = 32
ROWS = QR // BLOCKS
OWNERS = 8
HEADS_OWN = 8
SLOTS_OWN = 16
CHUNKS = 3
WIDTH = QK // CHUNKS
F32 = jnp.float32
BF16 = jnp.bfloat16


def rem(a, n):
    return lax.rem(a, jnp.int32(n))


def div(a, n):
    return lax.div(a, jnp.int32(n))


def dot_f32(a, b):
    return jnp.dot(a, b, precision=lax.Precision.HIGHEST, preferred_element_type=F32)


def kernel(
    index, grad, momentum, weight, k_weight, logits, slot_mask,
    momentum_out, weight_out, k_out,
    raw, packed, relay, direct, sibling, forward, forwarded, part, cross, heads, outgoing, arrived,
    mom, wgt, kwt, peaks, send_a, send_b, rows_a, rows_b, result, back,
    load_sem, state_sem, store_sem, s1_sem, fw_sem, s2_sem, relay_sem, direct_sem, sibling_sem,
    forwarded_sem, cross_sem, z_send, z_recv, x_send, x_recv, b_send, b_recv, l_send, l_recv,
):
    dp, z, ctx = lax.axis_index("dp"), lax.axis_index("owner"), lax.axis_index("context")
    core, y = rem(ctx, 2), rem(dp, 4)
    x = div(ctx, 2) * 2 + div(dp, 4)
    me = dp * 4 + ctx
    chip = x * 4 + y

    def at(x, y, c):
        return {"dp": rem(x, 2) * 4 + y, "context": div(x, 2) * 2 + c}

    def block(b):
        return {"dp": div(b, 4), "context": rem(b, 4)}

    def ring(half):
        return (x, y) if half == 0 else (y, x)

    def ring_device(half, r, c):
        return at(r, y, c) if half == 0 else at(x, r, c)

    def cross_device(half, q):
        return at(x, q, core) if half == 0 else at(q, y, core)

    def remote(src, dst, send, recv, device):
        copy = pltpu.make_async_remote_copy(
            src_ref=src, dst_ref=dst, send_sem=send, recv_sem=recv, device_id=device, device_id_type=MESH
        )
        copy.start()

    def wait(ref, sem):
        pltpu.make_async_copy(ref, ref, sem).wait()

    for k in range(CHUNKS):
        pltpu.make_async_copy(grad.at[:, k * WIDTH : (k + 1) * WIDTH, :], raw.at[k], load_sem.at[k]).start()
    loads = [
        pltpu.make_async_copy(momentum, mom, state_sem.at[0]),
        pltpu.make_async_copy(weight, wgt, state_sem.at[1]),
        pltpu.make_async_copy(k_weight, kwt, state_sem.at[2]),
    ]
    for copy in loads:
        copy.start()

    barrier = pltpu.get_barrier_semaphore()

    def greet(i, carry):
        pl.semaphore_signal(barrier, inc=1, device_id=block(rem(me + i, BLOCKS)), device_id_type=MESH)
        return carry

    def greet_z(i, carry):
        pl.semaphore_signal(barrier, inc=1, device_id={"owner": rem(z + i, OWNERS)}, device_id_type=MESH)
        return carry

    lax.fori_loop(1, BLOCKS, greet, 0)
    lax.fori_loop(1, OWNERS, greet_z, 0)

    row_at = lax.broadcasted_iota(jnp.int32, (384, 384), 0)
    column_at = lax.broadcasted_iota(jnp.int32, (384, 384), 1)
    eye = (row_at == column_at).astype(BF16)

    def pack(k):
        wait(raw.at[k], load_sem.at[k])
        for half in range(2):
            for group in range(4):
                block_in = raw[k, 4 * half : 4 * half + 4, :, 384 * group : 384 * group + 384]
                turned = lax.dot_general(
                    eye, block_in.reshape(4 * WIDTH, 384), (((1,), (1,)), ((), ())), preferred_element_type=F32
                ).astype(BF16)
                for i in range(8):
                    b = 8 * group + i
                    c_to, y_to, x_to = b % 2, (b // 4) % 4, (b // 2) % 2 * 2 + b // 16
                    r_to, q_to = (x_to, y_to) if half == 0 else (y_to, x_to)
                    for sub in range(2):
                        packed[k, half, r_to, c_to, sub, q_to] = turned[
                            ROWS * i : ROWS * i + ROWS, 128 * sub : 128 * sub + 128
                        ]

    def start_relays(k):
        for half in range(2):
            r, _ = ring(half)
            up, down, far = rem(r + 1, 4), rem(r + 3, 4), rem(r + 2, 4)
            for c in range(2):
                remote(packed.at[k, half, far, c, 0], relay.at[k, half, 0, core], s1_sem.at[k, half],
                       relay_sem.at[k, half], ring_device(half, up, c))
                remote(packed.at[k, half, far, c, 1], relay.at[k, half, 1, core], s1_sem.at[k, half],
                       relay_sem.at[k, half], ring_device(half, down, c))
            other = 1 - core
            here = at(x, y, other)
            remote(packed.at[k, half, up, other, 0], sibling.at[k, half, 0], s1_sem.at[k, half],
                   sibling_sem.at[k, half], here)
            remote(packed.at[k, half, down, other, 1], sibling.at[k, half, 1], s1_sem.at[k, half],
                   sibling_sem.at[k, half], here)
            remote(packed.at[k, half, r, other], sibling.at[k, half, pl.ds(2, 2)], s1_sem.at[k, half],
                   sibling_sem.at[k, half], here)

    def start_directs(k):
        for half in range(2):
            r, _ = ring(half)
            up, down = rem(r + 1, 4), rem(r + 3, 4)
            for c in range(2):
                remote(packed.at[k, half, up, c, 1], direct.at[k, half, 0, core], s1_sem.at[k, half],
                       direct_sem.at[k, half], ring_device(half, up, c))
                remote(packed.at[k, half, down, c, 0], direct.at[k, half, 1, core], s1_sem.at[k, half],
                       direct_sem.at[k, half], ring_device(half, down, c))

    def start_forwards(k):
        for half in range(2):
            r, _ = ring(half)
            up, down = rem(r + 1, 4), rem(r + 3, 4)
            wait(sibling.at[k, half], sibling_sem.at[k, half])
            wait(relay.at[k, half], relay_sem.at[k, half])
            for way, to in ((0, up), (1, down)):
                forward[k, half, way] = (
                    packed[k, half, to, core, way].astype(F32)
                    + sibling[k, half, way].astype(F32)
                    + relay[k, half, way, 0].astype(F32)
                    + relay[k, half, way, 1].astype(F32)
                )
                remote(forward.at[k, half, way], forwarded.at[k, half, way], fw_sem.at[k, half],
                       forwarded_sem.at[k, half], ring_device(half, to, core))

    def start_cross(k):
        for half in range(2):
            r, q = ring(half)
            wait(direct.at[k, half], direct_sem.at[k, half])
            wait(forwarded.at[k, half], forwarded_sem.at[k, half])
            for sub in range(2):
                total = (
                    packed[k, half, r, core, sub].astype(F32)
                    + sibling[k, half, 2 + sub].astype(F32)
                    + forwarded[k, half, sub]
                    + direct[k, half, 1 - sub, 0].astype(F32)
                    + direct[k, half, 1 - sub, 1].astype(F32)
                )
                for to in range(4):
                    part[k, half, to, sub] = total[to]
            for i in range(3):
                to = rem(q + 1 + i, 4)
                remote(part.at[k, half, to], cross.at[k, half, i], s2_sem.at[k, half],
                       cross_sem.at[k, half], cross_device(half, to))

    lane = lax.broadcasted_iota(jnp.int32, (ROWS, 128), 1)
    heads[HEADS_OWN] = jnp.zeros((ROWS, 128), F32)

    def start_owner(k):
        for half in range(2):
            _, q = ring(half)
            wait(cross.at[k, half], cross_sem.at[k, half])
            for sub in range(2):
                total = (
                    part[k, half, q, sub]
                    + cross[k, half, 0, sub]
                    + cross[k, half, 1, sub]
                    + cross[k, half, 2, sub]
                )
                pair = 2 * half + sub
                heads[2 * pair] = total
                heads[2 * pair + 1] = pltpu.roll(total, 64, 1)

        def fill(t, carry):
            outgoing[k, t] = jnp.where(lane < 64, heads[index[t]], heads[index[OWNERS + t]])
            return carry

        lax.fori_loop(0, OWNERS, fill, 0)
        for i in range(1, OWNERS):
            to = rem(z + i, OWNERS)
            remote(outgoing.at[k, to], arrived.at[k, z], z_send.at[k], z_recv.at[k], {"owner": to})
        arrived[k, z] = outgoing[k, z]

    def wait_owner(k):
        wait(arrived.at[k, pl.ds(0, OWNERS - 1)], z_recv.at[k])

    def start_rows(stage, source, target):
        def send(s, carry):
            mine = jnp.logical_and(s == chip, core == 0)

            @pl.when(jnp.logical_not(mine))
            def _():
                remote(source.at[s], target.at[me], x_send.at[stage], x_recv.at[stage], at(div(s, 4), rem(s, 4), 0))

            return carry

        lax.fori_loop(0, SLOTS_OWN, send, 0)

        @pl.when(core == 0)
        def _():
            target[me] = source[chip]

    pack(0)
    pl.semaphore_wait(barrier, BLOCKS - 1 + OWNERS - 1)
    start_relays(0)
    start_directs(0)
    peaks[ctx] = logits[...]
    for i in range(1, 4):
        remote(logits, peaks.at[ctx], l_send, l_recv, {"context": rem(ctx + i, 4)})
    pack(1)
    start_forwards(0)
    start_relays(1)
    start_directs(1)
    pack(2)
    start_cross(0)
    start_forwards(1)
    start_relays(2)
    start_directs(2)

    wait(peaks.at[pl.ds(0, 3)], l_recv)
    gamma = jnp.minimum(1.0, LOGIT_CAP / jnp.max(peaks[...], axis=0))
    occupied = jnp.sum(slot_mask[...], axis=1, keepdims=True) > 0.5
    slot_gamma = jnp.where(
        occupied, jnp.sum(slot_mask[...] * jnp.concatenate([gamma, gamma], axis=0), axis=1, keepdims=True), 1.0
    )
    rate = jnp.where(occupied, MOMENTUM_RATE, 1.0)
    keep = jnp.where(occupied, WEIGHT_KEEP, 1.0)
    step_size = jnp.where(occupied, 0.04 * math.sqrt(max(QR, QK)), 0.0)
    slot_root = jnp.sqrt(slot_gamma)
    home = lax.broadcasted_iota(jnp.int32, (8, 128), 1) == lax.broadcasted_iota(jnp.int32, (8, 128), 0) + 8 * z
    home_root = jnp.sqrt(jnp.sum(jnp.where(home, gamma, 0.0), axis=1, keepdims=True))
    loads[2].wait()
    for h in range(HEADS_OWN):
        kwt[h] = kwt[h] * home_root[h : h + 1, :]
    k_copy = pltpu.make_async_copy(kwt, k_out, store_sem.at[0])
    k_copy.start()

    start_owner(0)
    start_cross(1)
    start_forwards(2)
    start_owner(1)
    start_cross(2)
    loads[0].wait()
    wait_owner(0)
    wait_owner(1)
    for s in range(SLOTS_OWN):
        low, high = arrived[0, s // 2], arrived[1, s // 2]
        if s % 2 == 0:
            got = jnp.where(lane < 64, low, pltpu.roll(high, 64, 1))
        else:
            got = jnp.where(lane < 64, pltpu.roll(low, 64, 1), high)
        value = mom[s, :, 0:128] * rate[s : s + 1, :] + got
        mom[s, :, 0:128] = value
        send_a[s] = value.astype(BF16)
    start_rows(0, send_a, rows_a)
    start_owner(2)
    wait_owner(2)
    for s in range(SLOTS_OWN):
        got = arrived[2, s // 2]
        if s % 2 == 1:
            got = pltpu.roll(got, 64, 1)
        value = mom[s, :, 128:192] * rate[s : s + 1, :] + got[:, 0:64]
        mom[s, :, 128:192] = value
        send_b[s] = value.astype(BF16)
    start_rows(1, send_b, rows_b)
    m_copy = pltpu.make_async_copy(mom, momentum_out, store_sem.at[1])
    m_copy.start()

    @pl.when(core == 0)
    def _():
        wait(rows_a.at[pl.ds(0, BLOCKS - 1)], x_recv.at[0])
        wait(rows_b.at[pl.ds(0, BLOCKS - 1)], x_recv.at[1])
        whole = jnp.concatenate([rows_a[...].reshape(QR, 128), rows_b[...].reshape(QR, 64)], axis=1)
        square = (((0,), (0,)), ((), ()))
        gram = lax.dot_general(whole, whole, square, preferred_element_type=F32)
        diagonal = lax.broadcasted_iota(jnp.int32, (QK, QK), 0) == lax.broadcasted_iota(jnp.int32, (QK, QK), 1)
        square_sum = jnp.sum(jnp.sum(jnp.where(diagonal, gram, 0.0), axis=0, keepdims=True), axis=1, keepdims=True)
        scale = 1.0 / (jnp.sqrt(square_sum) + 1e-07)
        gram = gram * scale * scale
        for step in range(ITERS):
            polynomial = (QUINTIC_B * gram + QUINTIC_C * dot_f32(gram, gram)).astype(BF16)
            product = jnp.dot(whole, polynomial, preferred_element_type=F32)
            total = QUINTIC_A * whole.astype(F32) + product
            if step == 0:
                total = total * scale
            whole = total.astype(BF16)
            if step < ITERS - 1:
                gram = lax.dot_general(whole, whole, square, preferred_element_type=F32)
        result[...] = whole.reshape(BLOCKS, ROWS, QK)

        def send(i, carry):
            b = rem(me + i, BLOCKS)
            remote(result.at[b], back.at[chip], b_send, b_recv, block(b))
            return carry

        lax.fori_loop(1, BLOCKS, send, 0)
        back[chip] = result[me]

    loads[1].wait()

    @pl.when(core == 0)
    def _():
        wait(back.at[pl.ds(0, SLOTS_OWN - 1)], b_recv)

    @pl.when(core == 1)
    def _():
        wait(back, b_recv)

    for s in range(SLOTS_OWN):
        fresh = wgt[s] * keep[s : s + 1, :] - step_size[s : s + 1, :] * back[s].astype(F32)
        wgt[s, :, 0:128] = fresh[:, 0:128] * slot_root[s : s + 1, :]
        wgt[s, :, 128:192] = fresh[:, 128:192] * slot_gamma[s : s + 1, :]
    w_copy = pltpu.make_async_copy(wgt, weight_out, store_sem.at[2])
    w_copy.start()

    for k in range(CHUNKS):
        for half in range(2):
            wait(packed.at[k, half, pl.ds(0, 3)], s1_sem.at[k, half])
            wait(forward.at[k, half], fw_sem.at[k, half])
            wait(part.at[k, half, pl.ds(0, 3)], s2_sem.at[k, half])
        wait(outgoing.at[k, pl.ds(0, OWNERS - 1)], z_send.at[k])
    wait(peaks.at[pl.ds(0, 3)], l_send)

    @pl.when(core == 0)
    def _():
        wait(send_a.at[pl.ds(0, SLOTS_OWN - 1)], x_send.at[0])
        wait(send_b.at[pl.ds(0, SLOTS_OWN - 1)], x_send.at[1])
        wait(result.at[pl.ds(0, BLOCKS - 1)], b_send)

    @pl.when(core == 1)
    def _():
        wait(send_a, x_send.at[0])
        wait(send_b, x_send.at[1])

    k_copy.wait()
    m_copy.wait()
    w_copy.wait()


def routing(assignment, heads_own, per_source):
    target = assignment[:, 0]
    head_index = jnp.arange(target.shape[0], dtype=jnp.int32)
    source_block = head_index // heads_own
    earlier = (
        (source_block[None, :] == source_block[:, None])
        & (head_index[None, :] < head_index[:, None])
        & (target[None, :] == target[:, None])
    )
    position = jnp.sum(earlier.astype(jnp.int32), axis=1)
    return (target, position, source_block * per_source + position)


def body(grad_partials, assignment, momentum, q_weight, k_weight, max_logits):
    heads_own = grad_partials.shape[2]
    slots_own = momentum.shape[0]
    per_source = slots_own // OWNERS
    my_owner = lax.axis_index("owner")
    target, position, local_slot = routing(assignment, heads_own, per_source)
    slot_index = jnp.arange(slots_own, dtype=jnp.int32)
    slot_mask = ((target[None, :] == my_owner) & (local_slot[None, :] == slot_index[:, None])).astype(F32)
    slot_mask = jnp.pad(slot_mask, ((0, 0), (0, 64)))
    home = jnp.arange(64, dtype=jnp.int32)
    mine = (home // heads_own == my_owner)[None, :] & (
        (target[None, :] == slot_index[:, None] % OWNERS) & (position[None, :] == slot_index[:, None] // OWNERS)
    )
    local = jnp.where(slot_index[:, None] < OWNERS, home[None, :] % heads_own, (home[None, :] % heads_own) ^ 1)
    index = heads_own + jnp.sum(jnp.where(mine, local - heads_own, 0), axis=1)
    logits = jnp.broadcast_to(jnp.pad(max_logits, ((0, 0), (0, 64)), constant_values=LOGIT_CAP), (8, 128))
    turned = jnp.transpose(grad_partials[0], (1, 2, 0))
    any_space = pl.BlockSpec(memory_space=pl.ANY)
    vmem = pl.BlockSpec(memory_space=pltpu.VMEM)
    dma = pltpu.SemaphoreType.DMA
    wide = (4, ROWS, 128)
    return pl.pallas_call(
        kernel,
        out_shape=(
            jax.ShapeDtypeStruct(momentum.shape, F32),
            jax.ShapeDtypeStruct(q_weight.shape, F32),
            jax.ShapeDtypeStruct(k_weight.shape, F32),
        ),
        in_specs=[pl.BlockSpec(memory_space=pltpu.SMEM)] + [any_space] * 4 + [vmem] * 2,
        out_specs=(any_space,) * 3,
        scratch_shapes=[
            pltpu.VMEM((CHUNKS, HEADS_OWN, WIDTH, QR), BF16),
            pltpu.VMEM((CHUNKS, 2, 4, 2, 2) + wide, BF16),
            pltpu.VMEM((CHUNKS, 2, 2, 2) + wide, BF16),
            pltpu.VMEM((CHUNKS, 2, 2, 2) + wide, BF16),
            pltpu.VMEM((CHUNKS, 2, 4) + wide, BF16),
            pltpu.VMEM((CHUNKS, 2, 2) + wide, F32),
            pltpu.VMEM((CHUNKS, 2, 2) + wide, F32),
            pltpu.VMEM((CHUNKS, 2, 4, 2, ROWS, 128), F32),
            pltpu.VMEM((CHUNKS, 2, 3, 2, ROWS, 128), F32),
            pltpu.VMEM((HEADS_OWN + 1, ROWS, 128), F32),
            pltpu.VMEM((CHUNKS, OWNERS, ROWS, 128), F32),
            pltpu.VMEM((CHUNKS, OWNERS, ROWS, 128), F32),
            pltpu.VMEM(momentum.shape, F32),
            pltpu.VMEM(q_weight.shape, F32),
            pltpu.VMEM(k_weight.shape, F32),
            pltpu.VMEM((4, 8, 128), F32),
            pltpu.VMEM((SLOTS_OWN, ROWS, 128), BF16),
            pltpu.VMEM((SLOTS_OWN, ROWS, 64), BF16),
            pltpu.VMEM((BLOCKS, ROWS, 128), BF16),
            pltpu.VMEM((BLOCKS, ROWS, 64), BF16),
            pltpu.VMEM((BLOCKS, ROWS, QK), BF16),
            pltpu.VMEM((SLOTS_OWN, ROWS, QK), BF16),
            dma((CHUNKS,)),
            dma((3,)),
            dma((3,)),
            dma((CHUNKS, 2)),
            dma((CHUNKS, 2)),
            dma((CHUNKS, 2)),
            dma((CHUNKS, 2)),
            dma((CHUNKS, 2)),
            dma((CHUNKS, 2)),
            dma((CHUNKS, 2)),
            dma((CHUNKS, 2)),
            dma((CHUNKS,)),
            dma((CHUNKS,)),
            dma((2,)),
            dma((2,)),
            dma,
            dma,
            dma,
            dma,
        ],
        compiler_params=pltpu.CompilerParams(
            collective_id=0, has_side_effects=True, vmem_limit_bytes=56 * 1024 * 1024
        ),
    )(index, turned, momentum, q_weight, k_weight, logits, slot_mask)


def solution(mesh):
    placed = (
        P(("dp", "context"), None, "owner", None),
        P(),
        P("owner", ("dp", "context"), None),
        P("owner", ("dp", "context"), None),
        P("owner", ("dp", "context"), None),
        P("context", None),
    )
    return jax.shard_map(
        body,
        mesh=mesh,
        in_specs=placed,
        out_specs=(
            P("owner", ("dp", "context"), None),
            P("owner", ("dp", "context"), None),
            P("owner", ("dp", "context"), None),
        ),
        check_vma=False,
    )
```

time: 457 us -> 80.6 us (0.18)
  waiting for transfers between devices: 257 us -> 0 us
  blocking collectives: 77 us -> 0 us
  matrix products: 75.8 us -> 0 us
  Pallas kernels: 0 us -> 69.2 us
  between operations: 14.2 us -> 0.67 us
  starting transfers between devices: 8.69 us -> 0 us
  other arithmetic: 11.5 us -> 3.58 us
  local copies, waits for them, and re-layouts: 12.1 us -> 6.86 us
    reduce_scatter x1 -> x0, waiting for transfers between devices: 175 us -> none  [body(): lax.psum_scatter(partial_value.astype(jnp.float32), ('dp', 'context'), sc...]
    dot_general x7 -> x0, matrix products: 75.8 us -> none  [the longest x2 34.1 us: quintic(): jnp.einsum('nrk,nkl->nrl', whole, polynomial, preferred_element_type=jnp....]
    all_gather x1 -> x0, waiting for transfers between devices: 73.1 us -> none  [orthogonalize(): gathered = lax.all_gather(iterate, ('dp', 'context'), axis=1, tiled=True)]
    pallas_call x0 -> x1, Pallas kernels: none -> 69.2 us  [body(): pl.pallas_call(kernel, out_shape=(jax.ShapeDtypeStruct(momentum.shape, F3...]
    psum x1 -> x0, blocking collectives: 66.2 us -> none  [orthogonalize(): lax.psum(jnp.sum(matrix * matrix, axis=(1, 2)), ('dp', 'context'))]
    pmax x1 -> x0, blocking collectives: 10.9 us -> none  [body(): peak_logit = lax.pmax(max_logits[0], 'context')]
    all_to_all x1 -> x0, waiting for transfers between devices: 8.89 us -> none  [body(): lax.all_to_all(outgoing, 'owner', split_axis=0, concat_axis=0, tiled=True)]
    all_to_all x1 -> x0, starting transfers between devices: 8.62 us -> none  [body(): lax.all_to_all(outgoing, 'owner', split_axis=0, concat_axis=0, tiled=True)]
  transfers between devices with their start and end apart: 3 -> 0, of which waited for: 3 -> 0; matrix products, arithmetic and copies ran while one was open for 0% -> 0% of each run, Pallas kernels for 0% -> 0%
where the time goes in v1:
time: 80.6 us; the launch traced here: 80.3 us
  Pallas kernels  69.2 us (86%)
  local copies, waits for them, and re-layouts  6.86 us (9%)
  other arithmetic  3.58 us (4%)
    pallas_call x1, Pallas kernels, body(): pl.pallas_call(kernel, out_shape=(jax.ShapeDtypeStruct(momentum.shape, F3...  69.2 us
    unnamed x3, local copies, waits for them, and re-layouts  5.6 us

profile of v1, /device:TPU:1, one launch (start us, length us, event | category | flops | bytes accessed | tf_op | source)
XLA Modules:
  0.0 80.3 jit_solution(17556679030934407142)
XLA Ops:
  0.6 0.7 pad_bitcast_fusion
  1.3 0.9 %convert_reduce_fusion = s32[64]{0:T(128)S(1)} fusion(s32[64]{0:T(128)} %bitcast.8, s32[64]{0:T(128)S(1)} %and_select_fusion.3), kind=kLoop, calls=%fused_computation | loop fusion | flops 28608 | bytes 768 | tf_op jit(solution)/shard_map/reduce_sum | solution.py:384
  2.2 0.7 broadcast_compare_fusion
  2.9 0.8 %select_reduce_fusion = s32[16]{0:T(128)S(1)} fusion(s32[64]{0:T(128)S(1)} %get-tuple-element.6, s32[64]{0:T(128)S(1)} %get-tuple-element.5, s32[64]{0:T(128)S(1)} %convert_reduce_fusion, s32[64]{0:T(128)} %bitcast.9, s32[16]{0:T(128)S(1)} %get-tuple-element.7, s32[16]{0:T(128)S(1)} %get-tuple-element.8, pred[16]{0:T(512)(128)(4,1)S(1)} %iota_compare_fusion.2, ...), kind=kLoop, calls=%fused_computation.5 | loop fusion | flops 8176 | bytes 1296 | tf_op jit(solution)/shard_map/reduce_sum | solution.py:402
  3.8 0.5 broadcast_add_fusion.index
  4.3 0.6 broadcast_in_dim.53.logits
  4.9 0.6 pad_convert_fusion.slot_mask
  5.5 69.2 %shard_map.85 = (f32[16,48,192]{2,1,0:T(8,128)}, f32[16,48,192]{2,1,0:T(8,128)}, f32[8,16,128]{2,1,0:T(8,128)}) custom-call(s32[16]{0:T(128)} %broadcast_add_fusion.index, bf16[8,192,1536]{2,1,0:T(8,128)(2,1)} %bitcast.7, f32[16,48,192]{2,1,0:T(8,128)} %momentum.1, f32[16,48,192]{2,1,0:T(8,128)} %weight.1, f32[8,16,128]{2,1,0:T(8,128)} %k_weight.1, ...), custom_call_target="tpu_custom_call" | custom-call | tf_op jit(solution)/shard_map/pallas_call | solution.py:409
  74.7 2.1 %copy.12 = f32[16,48,192]{2,1,0:T(8,128)} copy(f32[16,48,192]{2,1,0:T(8,128)} %get-tuple-element.12) | data formatting | bytes 1179648
  76.8 2.1 %copy.13 = f32[16,48,192]{2,1,0:T(8,128)} copy(f32[16,48,192]{2,1,0:T(8,128)} %get-tuple-element.13) | data formatting | bytes 1179648
  78.9 1.5 %copy.14 = f32[8,16,128]{2,1,0:T(8,128)} copy(f32[8,16,128]{2,1,0:T(8,128)} %get-tuple-element.14) | data formatting | bytes 131072
  (6 shorter events, 0.0 us)

commit v2 on v1

--- a/solution.py
+++ b/solution.py
@@ -23,6 +23,7 @@
 ROWS = QR // BLOCKS
 OWNERS = 8
 HEADS_OWN = 8
+HEADS = 64
 SLOTS_OWN = 16
 CHUNKS = 3
 WIDTH = QK // CHUNKS
@@ -43,12 +44,14 @@
 
 
 def kernel(
-    index, grad, momentum, weight, k_weight, logits, slot_mask,
+    assignment, grad, momentum, weight, k_weight, logits,
     momentum_out, weight_out, k_out,
-    raw, packed, relay, direct, sibling, forward, forwarded, part, cross, heads, outgoing, arrived,
-    mom, wgt, kwt, peaks, send_a, send_b, rows_a, rows_b, result, back,
-    load_sem, state_sem, store_sem, s1_sem, fw_sem, s2_sem, relay_sem, direct_sem, sibling_sem,
-    forwarded_sem, cross_sem, z_send, z_recv, x_send, x_recv, b_send, b_recv, l_send, l_recv,
+    mom, wgt, kwt, raw, packed, relay, direct, sibling, forward, forwarded, part, cross_relay, cross_direct, cross_forward,
+    cross_forwarded, heads, outgoing, arrived, index, table, targets, logit_row, mine, peaks,
+    send_a, send_b, rows_a, rows_b, result, back,
+    load_sem, state_sem, s1_sem, fw_sem, s2_sem, relay_sem, direct_sem, sibling_sem, forwarded_sem,
+    cross_relay_sem, cross_direct_sem, cross_forwarded_sem,
+    z_send, z_recv, x_send, x_recv, b_send, b_recv, l_send, l_recv, store_sem,
 ):
     dp, z, ctx = lax.axis_index("dp"), lax.axis_index("owner"), lax.axis_index("context")
     core, y = rem(ctx, 2), rem(dp, 4)
@@ -86,6 +89,9 @@
         pltpu.make_async_copy(momentum, mom, state_sem.at[0]),
         pltpu.make_async_copy(weight, wgt, state_sem.at[1]),
         pltpu.make_async_copy(k_weight, kwt, state_sem.at[2]),
+        pltpu.make_async_copy(assignment, table, state_sem.at[3]),
+        pltpu.make_async_copy(assignment, targets, state_sem.at[4]),
+        pltpu.make_async_copy(logits, logit_row, state_sem.at[5]),
     ]
     for copy in loads:
         copy.start()
@@ -183,10 +189,23 @@
                 )
                 for to in range(4):
                     part[k, half, to, sub] = total[to]
-            for i in range(3):
-                to = rem(q + 1 + i, 4)
-                remote(part.at[k, half, to], cross.at[k, half, i], s2_sem.at[k, half],
-                       cross_sem.at[k, half], cross_device(half, to))
+            up, down, far = rem(q + 1, 4), rem(q + 3, 4), rem(q + 2, 4)
+            for way, to in ((0, up), (1, down)):
+                remote(part.at[k, half, far, way], cross_relay.at[k, half, way], s2_sem.at[k, half],
+                       cross_relay_sem.at[k, half], cross_device(half, to))
+            for way, to in ((0, up), (1, down)):
+                remote(part.at[k, half, to, 1 - way], cross_direct.at[k, half, way], s2_sem.at[k, half],
+                       cross_direct_sem.at[k, half], cross_device(half, to))
+
+    def start_cross_forwards(k):
+        for half in range(2):
+            _, q = ring(half)
+            up, down = rem(q + 1, 4), rem(q + 3, 4)
+            wait(cross_relay.at[k, half], cross_relay_sem.at[k, half])
+            for way, to in ((0, up), (1, down)):
+                cross_forward[k, half, way] = part[k, half, to, way] + cross_relay[k, half, way]
+                remote(cross_forward.at[k, half, way], cross_forwarded.at[k, half, way], s2_sem.at[k, half],
+                       cross_forwarded_sem.at[k, half], cross_device(half, to))
 
     lane = lax.broadcasted_iota(jnp.int32, (ROWS, 128), 1)
     heads[HEADS_OWN] = jnp.zeros((ROWS, 128), F32)
@@ -194,14 +213,10 @@
     def start_owner(k):
         for half in range(2):
             _, q = ring(half)
-            wait(cross.at[k, half], cross_sem.at[k, half])
+            wait(cross_direct.at[k, half], cross_direct_sem.at[k, half])
+            wait(cross_forwarded.at[k, half], cross_forwarded_sem.at[k, half])
             for sub in range(2):
-                total = (
-                    part[k, half, q, sub]
-                    + cross[k, half, 0, sub]
-                    + cross[k, half, 1, sub]
-                    + cross[k, half, 2, sub]
-                )
+                total = part[k, half, q, sub] + cross_forwarded[k, half, sub] + cross_direct[k, half, 1 - sub]
                 pair = 2 * half + sub
                 heads[2 * pair] = total
                 heads[2 * pair + 1] = pltpu.roll(total, 64, 1)
@@ -239,9 +254,12 @@
     pl.semaphore_wait(barrier, BLOCKS - 1 + OWNERS - 1)
     start_relays(0)
     start_directs(0)
-    peaks[ctx] = logits[...]
+    loads[5].wait()
+    row = logit_row[...]
+    mine[...] = jnp.broadcast_to(jnp.concatenate([row, row], axis=1), (8, 128))
+    peaks[ctx] = mine[...]
     for i in range(1, 4):
-        remote(logits, peaks.at[ctx], l_send, l_recv, {"context": rem(ctx + i, 4)})
+        remote(mine, peaks.at[ctx], l_send, l_recv, {"context": rem(ctx + i, 4)})
     pack(1)
     start_forwards(0)
     start_relays(1)
@@ -251,12 +269,37 @@
     start_forwards(1)
     start_relays(2)
     start_directs(2)
-
+    start_cross_forwards(0)
+
+    loads[3].wait()
+    named = [table[0, HEADS_OWN * z + i] for i in range(HEADS_OWN)]
+    for t in range(OWNERS):
+        first, beside, second = jnp.int32(HEADS_OWN), jnp.int32(HEADS_OWN), jnp.int32(HEADS_OWN)
+        for i in reversed(range(HEADS_OWN)):
+            hit = named[i] == t
+            second = jnp.where(hit, beside, second)
+            beside = jnp.where(hit, i ^ 1, beside)
+            first = jnp.where(hit, i, first)
+        index[t] = first
+        index[OWNERS + t] = second
+
+    loads[4].wait()
+    along = jnp.broadcast_to(targets[...].astype(F32), (HEADS, HEADS))
+    head_row = lax.broadcasted_iota(jnp.int32, (HEADS, HEADS), 0)
+    head_lane = lax.broadcasted_iota(jnp.int32, (HEADS, HEADS), 1)
+    down_column = jnp.sum(jnp.where(head_row == head_lane, along, 0.0), axis=1, keepdims=True)
+    earlier = (down_column == along) & (div(head_row, 8) == div(head_lane, 8)) & (head_row < head_lane)
+    position = jnp.sum(jnp.where(earlier, 1.0, 0.0), axis=0, keepdims=True)
+    slot_row = lax.broadcasted_iota(jnp.int32, (SLOTS_OWN, HEADS), 0)
+    slot_lane = lax.broadcasted_iota(jnp.int32, (SLOTS_OWN, HEADS), 1)
+    in_slot = (along[0:SLOTS_OWN] == z.astype(F32)) & (
+        (div(slot_lane, 8) * 2).astype(F32) + position == slot_row.astype(F32)
+    )
     wait(peaks.at[pl.ds(0, 3)], l_recv)
     gamma = jnp.minimum(1.0, LOGIT_CAP / jnp.max(peaks[...], axis=0))
-    occupied = jnp.sum(slot_mask[...], axis=1, keepdims=True) > 0.5
+    occupied = jnp.sum(jnp.where(in_slot, 1.0, 0.0), axis=1, keepdims=True) > 0.5
     slot_gamma = jnp.where(
-        occupied, jnp.sum(slot_mask[...] * jnp.concatenate([gamma, gamma], axis=0), axis=1, keepdims=True), 1.0
+        occupied, jnp.sum(jnp.where(in_slot, gamma[0:1, 0:HEADS], 0.0), axis=1, keepdims=True), 1.0
     )
     rate = jnp.where(occupied, MOMENTUM_RATE, 1.0)
     keep = jnp.where(occupied, WEIGHT_KEEP, 1.0)
@@ -267,14 +310,21 @@
     loads[2].wait()
     for h in range(HEADS_OWN):
         kwt[h] = kwt[h] * home_root[h : h + 1, :]
-    k_copy = pltpu.make_async_copy(kwt, k_out, store_sem.at[0])
-    k_copy.start()
-
-    start_owner(0)
+    stores = [
+        pltpu.make_async_copy(mom, momentum_out, store_sem.at[0]),
+        pltpu.make_async_copy(wgt, weight_out, store_sem.at[1]),
+        pltpu.make_async_copy(kwt, k_out, store_sem.at[2]),
+    ]
+    stores[2].start()
+
     start_cross(1)
     start_forwards(2)
+    start_owner(0)
+    start_cross_forwards(1)
+    start_cross(2)
     start_owner(1)
-    start_cross(2)
+    start_cross_forwards(2)
+    start_owner(2)
     loads[0].wait()
     wait_owner(0)
     wait_owner(1)
@@ -288,7 +338,6 @@
         mom[s, :, 0:128] = value
         send_a[s] = value.astype(BF16)
     start_rows(0, send_a, rows_a)
-    start_owner(2)
     wait_owner(2)
     for s in range(SLOTS_OWN):
         got = arrived[2, s // 2]
@@ -296,16 +345,17 @@
             got = pltpu.roll(got, 64, 1)
         value = mom[s, :, 128:192] * rate[s : s + 1, :] + got[:, 0:64]
         mom[s, :, 128:192] = value
-        send_b[s] = value.astype(BF16)
+        send_b[s] = jnp.concatenate([value[0:24], value[24:48]], axis=1).astype(BF16)
     start_rows(1, send_b, rows_b)
-    m_copy = pltpu.make_async_copy(mom, momentum_out, store_sem.at[1])
-    m_copy.start()
+    stores[0].start()
 
     @pl.when(core == 0)
     def _():
         wait(rows_a.at[pl.ds(0, BLOCKS - 1)], x_recv.at[0])
         wait(rows_b.at[pl.ds(0, BLOCKS - 1)], x_recv.at[1])
-        whole = jnp.concatenate([rows_a[...].reshape(QR, 128), rows_b[...].reshape(QR, 64)], axis=1)
+        tail = rows_b[...].astype(F32)
+        tail = jnp.concatenate([tail[:, :, 0:64], tail[:, :, 64:128]], axis=1).astype(BF16)
+        whole = jnp.concatenate([rows_a[...].reshape(QR, 128), tail.reshape(QR, 64)], axis=1)
         square = (((0,), (0,)), ((), ()))
         gram = lax.dot_general(whole, whole, square, preferred_element_type=F32)
         diagonal = lax.broadcasted_iota(jnp.int32, (QK, QK), 0) == lax.broadcasted_iota(jnp.int32, (QK, QK), 1)
@@ -318,10 +368,12 @@
             total = QUINTIC_A * whole.astype(F32) + product
             if step == 0:
                 total = total * scale
-            whole = total.astype(BF16)
             if step < ITERS - 1:
+                whole = total.astype(BF16)
                 gram = lax.dot_general(whole, whole, square, preferred_element_type=F32)
-        result[...] = whole.reshape(BLOCKS, ROWS, QK)
+        result[:, 0:ROWS, :] = total[:, 0:128].astype(BF16).reshape(BLOCKS, ROWS, 128)
+        tail = total[:, 128:192].reshape(BLOCKS, ROWS, 64)
+        result[:, ROWS:72, :] = jnp.concatenate([tail[:, 0:24], tail[:, 24:48]], axis=2).astype(BF16)
 
         def send(i, carry):
             b = rem(me + i, BLOCKS)
@@ -342,11 +394,13 @@
         wait(back, b_recv)
 
     for s in range(SLOTS_OWN):
-        fresh = wgt[s] * keep[s : s + 1, :] - step_size[s : s + 1, :] * back[s].astype(F32)
-        wgt[s, :, 0:128] = fresh[:, 0:128] * slot_root[s : s + 1, :]
-        wgt[s, :, 128:192] = fresh[:, 128:192] * slot_gamma[s : s + 1, :]
-    w_copy = pltpu.make_async_copy(wgt, weight_out, store_sem.at[2])
-    w_copy.start()
+        kept, taken = keep[s : s + 1, :], step_size[s : s + 1, :]
+        fresh = back[s].astype(F32)
+        wgt[s, :, 0:128] = (wgt[s, :, 0:128] * kept - taken * fresh[0:ROWS]) * slot_root[s : s + 1, :]
+        tail = jnp.concatenate([fresh[ROWS:72, 0:64], fresh[ROWS:72, 64:128]], axis=0)
+        wgt[s, :, 128:192] = (wgt[s, :, 128:192] * kept - taken * tail) * slot_gamma[s : s + 1, :]
+
+    stores[1].start()
 
     for k in range(CHUNKS):
         for half in range(2):
@@ -367,55 +421,42 @@
         wait(send_a, x_send.at[0])
         wait(send_b, x_send.at[1])
 
-    k_copy.wait()
-    m_copy.wait()
-    w_copy.wait()
-
-
-def routing(assignment, heads_own, per_source):
-    target = assignment[:, 0]
-    head_index = jnp.arange(target.shape[0], dtype=jnp.int32)
-    source_block = head_index // heads_own
-    earlier = (
-        (source_block[None, :] == source_block[:, None])
-        & (head_index[None, :] < head_index[:, None])
-        & (target[None, :] == target[:, None])
-    )
-    position = jnp.sum(earlier.astype(jnp.int32), axis=1)
-    return (target, position, source_block * per_source + position)
+    for copy in stores:
+        copy.wait()
+
+
+def place(mom, wgt, kwt, momentum_out, weight_out, k_out, sem):
+    copies = [
+        pltpu.make_async_copy(mom, momentum_out, sem.at[0]),
+        pltpu.make_async_copy(wgt, weight_out, sem.at[1]),
+        pltpu.make_async_copy(kwt, k_out, sem.at[2]),
+    ]
+    for copy in copies:
+        copy.start()
+    for copy in copies:
+        copy.wait()
 
 
 def body(grad_partials, assignment, momentum, q_weight, k_weight, max_logits):
-    heads_own = grad_partials.shape[2]
-    slots_own = momentum.shape[0]
-    per_source = slots_own // OWNERS
-    my_owner = lax.axis_index("owner")
-    target, position, local_slot = routing(assignment, heads_own, per_source)
-    slot_index = jnp.arange(slots_own, dtype=jnp.int32)
-    slot_mask = ((target[None, :] == my_owner) & (local_slot[None, :] == slot_index[:, None])).astype(F32)
-    slot_mask = jnp.pad(slot_mask, ((0, 0), (0, 64)))
-    home = jnp.arange(64, dtype=jnp.int32)
-    mine = (home // heads_own == my_owner)[None, :] & (
-        (target[None, :] == slot_index[:, None] % OWNERS) & (position[None, :] == slot_index[:, None] // OWNERS)
-    )
-    local = jnp.where(slot_index[:, None] < OWNERS, home[None, :] % heads_own, (home[None, :] % heads_own) ^ 1)
-    index = heads_own + jnp.sum(jnp.where(mine, local - heads_own, 0), axis=1)
-    logits = jnp.broadcast_to(jnp.pad(max_logits, ((0, 0), (0, 64)), constant_values=LOGIT_CAP), (8, 128))
     turned = jnp.transpose(grad_partials[0], (1, 2, 0))
-    any_space = pl.BlockSpec(memory_space=pl.ANY)
+    hbm = pl.BlockSpec(memory_space=pltpu.HBM)
     vmem = pl.BlockSpec(memory_space=pltpu.VMEM)
     dma = pltpu.SemaphoreType.DMA
     wide = (4, ROWS, 128)
-    return pl.pallas_call(
+    outs = (
+        jax.ShapeDtypeStruct(momentum.shape, F32),
+        jax.ShapeDtypeStruct(q_weight.shape, F32),
+        jax.ShapeDtypeStruct(k_weight.shape, F32),
+    )
+    made = pl.pallas_call(
         kernel,
-        out_shape=(
-            jax.ShapeDtypeStruct(momentum.shape, F32),
-            jax.ShapeDtypeStruct(q_weight.shape, F32),
-            jax.ShapeDtypeStruct(k_weight.shape, F32),
-        ),
-        in_specs=[pl.BlockSpec(memory_space=pltpu.SMEM)] + [any_space] * 4 + [vmem] * 2,
-        out_specs=(any_space,) * 3,
+        out_shape=outs,
+        in_specs=[hbm] * 6,
+        out_specs=(hbm,) * 3,
         scratch_shapes=[
+            pltpu.VMEM(momentum.shape, F32),
+            pltpu.VMEM(q_weight.shape, F32),
+            pltpu.VMEM(k_weight.shape, F32),
             pltpu.VMEM((CHUNKS, HEADS_OWN, WIDTH, QR), BF16),
             pltpu.VMEM((CHUNKS, 2, 4, 2, 2) + wide, BF16),
             pltpu.VMEM((CHUNKS, 2, 2, 2) + wide, BF16),
@@ -424,44 +465,41 @@
             pltpu.VMEM((CHUNKS, 2, 2) + wide, F32),
             pltpu.VMEM((CHUNKS, 2, 2) + wide, F32),
             pltpu.VMEM((CHUNKS, 2, 4, 2, ROWS, 128), F32),
-            pltpu.VMEM((CHUNKS, 2, 3, 2, ROWS, 128), F32),
+            pltpu.VMEM((CHUNKS, 2, 2, ROWS, 128), F32),
+            pltpu.VMEM((CHUNKS, 2, 2, ROWS, 128), F32),
+            pltpu.VMEM((CHUNKS, 2, 2, ROWS, 128), F32),
+            pltpu.VMEM((CHUNKS, 2, 2, ROWS, 128), F32),
             pltpu.VMEM((HEADS_OWN + 1, ROWS, 128), F32),
             pltpu.VMEM((CHUNKS, OWNERS, ROWS, 128), F32),
             pltpu.VMEM((CHUNKS, OWNERS, ROWS, 128), F32),
-            pltpu.VMEM(momentum.shape, F32),
-            pltpu.VMEM(q_weight.shape, F32),
-            pltpu.VMEM(k_weight.shape, F32),
+            pltpu.SMEM((2 * OWNERS,), jnp.int32),
+            pltpu.SMEM((1, HEADS), jnp.int32),
+            pltpu.VMEM((1, HEADS), jnp.int32),
+            pltpu.VMEM((1, HEADS), F32),
+            pltpu.VMEM((8, 128), F32),
             pltpu.VMEM((4, 8, 128), F32),
             pltpu.VMEM((SLOTS_OWN, ROWS, 128), BF16),
-            pltpu.VMEM((SLOTS_OWN, ROWS, 64), BF16),
+            pltpu.VMEM((SLOTS_OWN, 24, 128), BF16),
             pltpu.VMEM((BLOCKS, ROWS, 128), BF16),
-            pltpu.VMEM((BLOCKS, ROWS, 64), BF16),
-            pltpu.VMEM((BLOCKS, ROWS, QK), BF16),
-            pltpu.VMEM((SLOTS_OWN, ROWS, QK), BF16),
+            pltpu.VMEM((BLOCKS, 24, 128), BF16),
+            pltpu.VMEM((BLOCKS, 72, 128), BF16),
+            pltpu.VMEM((SLOTS_OWN, 72, 128), BF16),
             dma((CHUNKS,)),
-            dma((3,)),
-            dma((3,)),
-            dma((CHUNKS, 2)),
-            dma((CHUNKS, 2)),
-            dma((CHUNKS, 2)),
-            dma((CHUNKS, 2)),
-            dma((CHUNKS, 2)),
-            dma((CHUNKS, 2)),
-            dma((CHUNKS, 2)),
-            dma((CHUNKS, 2)),
-            dma((CHUNKS,)),
-            dma((CHUNKS,)),
-            dma((2,)),
-            dma((2,)),
-            dma,
-            dma,
-            dma,
-            dma,
-        ],
+            dma((6,)),
+        ]
+        + [dma((CHUNKS, 2))] * 10
+        + [dma((CHUNKS,)), dma((CHUNKS,)), dma((2,)), dma((2,)), dma, dma, dma, dma, dma((3,))],
         compiler_params=pltpu.CompilerParams(
             collective_id=0, has_side_effects=True, vmem_limit_bytes=56 * 1024 * 1024
         ),
-    )(index, turned, momentum, q_weight, k_weight, logits, slot_mask)
+    )(assignment.reshape(1, HEADS), turned, momentum, q_weight, k_weight, max_logits)
+    return pl.pallas_call(
+        place,
+        out_shape=outs,
+        in_specs=[vmem] * 3,
+        out_specs=(hbm,) * 3,
+        scratch_shapes=[dma((3,))],
+    )(*made)
 
 
 def solution(mesh):

time: 80.6 us -> 70.1 us (0.87)
  local copies, waits for them, and re-layouts: 6.86 us -> 0 us
  other arithmetic: 3.58 us -> 0 us
    unnamed x3 -> x0, local copies, waits for them, and re-layouts: 5.6 us -> none
    reduce_sum x2 -> x0, other arithmetic: 1.76 us -> none  [the longest x1 0.91 us: routing(): position = jnp.sum(earlier.astype(jnp.int32), axis=1)]
    broadcast_in_dim x2 -> x0, local copies, waits for them, and re-layouts: 1.25 us -> none  [body(): jnp.broadcast_to(jnp.pad(max_logits, ((0, 0), (0, 64)), constant_values=L...]
    pallas_call x1 -> x2, Pallas kernels: 69.2 us -> 69.3 us  [the longest x1 66.8 us: body(): pl.pallas_call(kernel, out_shape=outs, in_specs=[hbm] * 6, out_specs=(hbm...]
where the time goes in v2:
time: 70.1 us; the launch traced here: 70 us
  Pallas kernels  69.3 us (99%)
    pallas_call x1, Pallas kernels, body(): pl.pallas_call(kernel, out_shape=outs, in_specs=[hbm] * 6, out_specs=(hbm...  66.8 us
    pallas_call x1, Pallas kernels, body(): pl.pallas_call(place, out_shape=outs, in_specs=[vmem] * 3, out_specs=(hbm...  2.55 us

profile of v2, /device:TPU:1, one launch (start us, length us, event | category | flops | bytes accessed | tf_op | source)
XLA Modules:
  0.0 70.0 jit_solution(12279249779053043937)
XLA Ops:
  0.6 66.8 %shard_map.85 = (f32[16,48,192]{2,1,0:T(8,128)}, f32[16,48,192]{2,1,0:T(8,128)}, f32[8,16,128]{2,1,0:T(8,128)}) custom-call(s32[1,64]{1,0:T(1,128)} %bitcast.5, bf16[8,192,1536]{2,1,0:T(8,128)(2,1)} %bitcast.4, f32[16,48,192]{2,1,0:T(8,128)} %momentum.1, f32[16,48,192]{2,1,0:T(8,128)} %weight.1, f32[8,16,128]{2,1,0:T(8,128)} %k_weight.1, f32[1,64]{1,0:T(1,128)} %logits.1), custom_call_target="tpu_custom_call" | custom-call | tf_op jit(solution)/shard_map/pallas_call | solution.py:451
  67.4 2.5 %shard_map.86 = (f32[16,48,192]{2,1,0:T(8,128)}, f32[16,48,192]{2,1,0:T(8,128)}, f32[8,16,128]{2,1,0:T(8,128)}) custom-call(f32[16,48,192]{2,1,0:T(8,128)} %get-tuple-element.6.mom, f32[16,48,192]{2,1,0:T(8,128)} %get-tuple-element.7.wgt, f32[8,16,128]{2,1,0:T(8,128)} %get-tuple-element.8.kwt), custom_call_target="tpu_custom_call" | custom-call | tf_op jit(solution)/shard_map/pallas_call | solution.py:496

commit v3 on v2

--- a/solution.py
+++ b/solution.py
@@ -44,14 +44,14 @@
 
 
 def kernel(
-    assignment, grad, momentum, weight, k_weight, logits,
-    momentum_out, weight_out, k_out,
-    mom, wgt, kwt, raw, packed, relay, direct, sibling, forward, forwarded, part, cross_relay, cross_direct, cross_forward,
+    assignment, grad, momentum, k_weight, logits,
+    momentum_out, k_out, scale_out, back,
+    mom, kwt, scales, raw, packed, relay, direct, sibling, forward, forwarded, part, cross_relay, cross_direct, cross_forward,
     cross_forwarded, heads, outgoing, arrived, index, table, targets, logit_row, mine, peaks,
-    send_a, send_b, rows_a, rows_b, result, back,
+    send_a, send_b, rows_a, rows_b, gram_mine, gram_other, iterate, result,
     load_sem, state_sem, s1_sem, fw_sem, s2_sem, relay_sem, direct_sem, sibling_sem, forwarded_sem,
     cross_relay_sem, cross_direct_sem, cross_forwarded_sem,
-    z_send, z_recv, x_send, x_recv, b_send, b_recv, l_send, l_recv, store_sem,
+    z_send, z_recv, x_send, x_recv, g_send, g_recv, b_send, b_recv, l_send, l_recv, store_sem,
 ):
     dp, z, ctx = lax.axis_index("dp"), lax.axis_index("owner"), lax.axis_index("context")
     core, y = rem(ctx, 2), rem(dp, 4)
@@ -87,11 +87,10 @@
         pltpu.make_async_copy(grad.at[:, k * WIDTH : (k + 1) * WIDTH, :], raw.at[k], load_sem.at[k]).start()
     loads = [
         pltpu.make_async_copy(momentum, mom, state_sem.at[0]),
-        pltpu.make_async_copy(weight, wgt, state_sem.at[1]),
-        pltpu.make_async_copy(k_weight, kwt, state_sem.at[2]),
-        pltpu.make_async_copy(assignment, table, state_sem.at[3]),
-        pltpu.make_async_copy(assignment, targets, state_sem.at[4]),
-        pltpu.make_async_copy(logits, logit_row, state_sem.at[5]),
+        pltpu.make_async_copy(k_weight, kwt, state_sem.at[1]),
+        pltpu.make_async_copy(assignment, table, state_sem.at[2]),
+        pltpu.make_async_copy(assignment, targets, state_sem.at[3]),
+        pltpu.make_async_copy(logits, logit_row, state_sem.at[4]),
     ]
     for copy in loads:
         copy.start()
@@ -235,43 +234,38 @@
         wait(arrived.at[k, pl.ds(0, OWNERS - 1)], z_recv.at[k])
 
     def start_rows(stage, source, target):
-        def send(s, carry):
-            mine = jnp.logical_and(s == chip, core == 0)
-
-            @pl.when(jnp.logical_not(mine))
-            def _():
-                remote(source.at[s], target.at[me], x_send.at[stage], x_recv.at[stage], at(div(s, 4), rem(s, 4), 0))
-
+        def send(i, carry):
+            s = rem(chip + i, SLOTS_OWN)
+            remote(source.at[s], target.at[div(me, 2)], x_send.at[stage], x_recv.at[stage],
+                   at(div(s, 4), rem(s, 4), core))
             return carry
 
-        lax.fori_loop(0, SLOTS_OWN, send, 0)
-
-        @pl.when(core == 0)
-        def _():
-            target[me] = source[chip]
+        lax.fori_loop(1, SLOTS_OWN, send, 0)
+        target[div(me, 2)] = source[chip]
 
     pack(0)
     pl.semaphore_wait(barrier, BLOCKS - 1 + OWNERS - 1)
     start_relays(0)
+    pack(1)
+    start_relays(1)
     start_directs(0)
-    loads[5].wait()
+    start_forwards(0)
+    loads[4].wait()
     row = logit_row[...]
     mine[...] = jnp.broadcast_to(jnp.concatenate([row, row], axis=1), (8, 128))
     peaks[ctx] = mine[...]
     for i in range(1, 4):
         remote(mine, peaks.at[ctx], l_send, l_recv, {"context": rem(ctx + i, 4)})
-    pack(1)
-    start_forwards(0)
-    start_relays(1)
+    pack(2)
+    start_relays(2)
+    start_cross(0)
     start_directs(1)
-    pack(2)
-    start_cross(0)
     start_forwards(1)
-    start_relays(2)
+    start_cross_forwards(0)
     start_directs(2)
-    start_cross_forwards(0)
-
-    loads[3].wait()
+    start_forwards(2)
+
+    loads[2].wait()
     named = [table[0, HEADS_OWN * z + i] for i in range(HEADS_OWN)]
     for t in range(OWNERS):
         first, beside, second = jnp.int32(HEADS_OWN), jnp.int32(HEADS_OWN), jnp.int32(HEADS_OWN)
@@ -283,7 +277,7 @@
         index[t] = first
         index[OWNERS + t] = second
 
-    loads[4].wait()
+    loads[3].wait()
     along = jnp.broadcast_to(targets[...].astype(F32), (HEADS, HEADS))
     head_row = lax.broadcasted_iota(jnp.int32, (HEADS, HEADS), 0)
     head_lane = lax.broadcasted_iota(jnp.int32, (HEADS, HEADS), 1)
@@ -307,19 +301,23 @@
     slot_root = jnp.sqrt(slot_gamma)
     home = lax.broadcasted_iota(jnp.int32, (8, 128), 1) == lax.broadcasted_iota(jnp.int32, (8, 128), 0) + 8 * z
     home_root = jnp.sqrt(jnp.sum(jnp.where(home, gamma, 0.0), axis=1, keepdims=True))
-    loads[2].wait()
+    loads[1].wait()
     for h in range(HEADS_OWN):
         kwt[h] = kwt[h] * home_root[h : h + 1, :]
     stores = [
         pltpu.make_async_copy(mom, momentum_out, store_sem.at[0]),
-        pltpu.make_async_copy(wgt, weight_out, store_sem.at[1]),
-        pltpu.make_async_copy(kwt, k_out, store_sem.at[2]),
+        pltpu.make_async_copy(kwt, k_out, store_sem.at[1]),
+        pltpu.make_async_copy(scales, scale_out, store_sem.at[2]),
     ]
+    stores[1].start()
+    scale_lane = lax.broadcasted_iota(jnp.int32, (SLOTS_OWN, 128), 1)
+    scales[...] = jnp.where(
+        scale_lane == 0, keep, jnp.where(scale_lane == 1, step_size, jnp.where(scale_lane == 2, slot_root, slot_gamma))
+    )
     stores[2].start()
 
+    start_owner(0)
     start_cross(1)
-    start_forwards(2)
-    start_owner(0)
     start_cross_forwards(1)
     start_cross(2)
     start_owner(1)
@@ -349,58 +347,59 @@
     start_rows(1, send_b, rows_b)
     stores[0].start()
 
-    @pl.when(core == 0)
-    def _():
-        wait(rows_a.at[pl.ds(0, BLOCKS - 1)], x_recv.at[0])
-        wait(rows_b.at[pl.ds(0, BLOCKS - 1)], x_recv.at[1])
-        tail = rows_b[...].astype(F32)
-        tail = jnp.concatenate([tail[:, :, 0:64], tail[:, :, 64:128]], axis=1).astype(BF16)
-        whole = jnp.concatenate([rows_a[...].reshape(QR, 128), tail.reshape(QR, 64)], axis=1)
-        square = (((0,), (0,)), ((), ()))
-        gram = lax.dot_general(whole, whole, square, preferred_element_type=F32)
-        diagonal = lax.broadcasted_iota(jnp.int32, (QK, QK), 0) == lax.broadcasted_iota(jnp.int32, (QK, QK), 1)
-        square_sum = jnp.sum(jnp.sum(jnp.where(diagonal, gram, 0.0), axis=0, keepdims=True), axis=1, keepdims=True)
-        scale = 1.0 / (jnp.sqrt(square_sum) + 1e-07)
-        gram = gram * scale * scale
-        for step in range(ITERS):
-            polynomial = (QUINTIC_B * gram + QUINTIC_C * dot_f32(gram, gram)).astype(BF16)
-            product = jnp.dot(whole, polynomial, preferred_element_type=F32)
-            total = QUINTIC_A * whole.astype(F32) + product
-            if step == 0:
-                total = total * scale
-            if step < ITERS - 1:
-                whole = total.astype(BF16)
-                gram = lax.dot_general(whole, whole, square, preferred_element_type=F32)
-        result[:, 0:ROWS, :] = total[:, 0:128].astype(BF16).reshape(BLOCKS, ROWS, 128)
-        tail = total[:, 128:192].reshape(BLOCKS, ROWS, 64)
-        result[:, ROWS:72, :] = jnp.concatenate([tail[:, 0:24], tail[:, 24:48]], axis=2).astype(BF16)
+    others = pl.ds(0, SLOTS_OWN - 1)
+    wait(rows_a.at[others], x_recv.at[0])
+    wait(rows_b.at[others], x_recv.at[1])
+    tail = rows_b[...].astype(F32)
+    tail = jnp.concatenate([tail[:, :, 0:64], tail[:, :, 64:128]], axis=1).astype(BF16)
+    whole = jnp.concatenate([rows_a[...].reshape(QR // 2, 128), tail.reshape(QR // 2, 64)], axis=1)
+    gram_mine[...] = lax.dot_general(whole, whole, (((0,), (0,)), ((), ())), preferred_element_type=F32)
+    remote(gram_mine, gram_other, g_send, g_recv, at(x, y, 1 - core))
+    wait(gram_other, g_recv)
+    gram = gram_mine[...] + gram_other[...]
+    diagonal = lax.broadcasted_iota(jnp.int32, (QK, QK), 0) == lax.broadcasted_iota(jnp.int32, (QK, QK), 1)
+    square_sum = jnp.sum(jnp.sum(jnp.where(diagonal, gram, 0.0), axis=0, keepdims=True), axis=1, keepdims=True)
+    scale = 1.0 / (jnp.sqrt(square_sum) + 1e-07)
+    gram = gram * scale * scale
+    for step in range(ITERS - 1):
+        polynomial = (QUINTIC_B * gram + QUINTIC_C * dot_f32(gram, gram)).astype(BF16)
+        total = QUINTIC_A * whole.astype(F32) + jnp.dot(whole, polynomial, preferred_element_type=F32)
+        if step == 0:
+            total = total * scale
+        whole = total.astype(BF16)
+        factor = polynomial.astype(F32) + jnp.where(diagonal, QUINTIC_A, 0.0)
+        gram = dot_f32(factor, dot_f32(gram, factor))
+    iterate[...] = whole
+    polynomial = (QUINTIC_B * gram + QUINTIC_C * dot_f32(gram, gram)).astype(BF16)
+
+    def finish_group(n, carry):
+        group = rem(n + x, 4)
+        rows = iterate[pl.ds(pl.multiple_of(group * 192, 192), 192), :]
+        total = QUINTIC_A * rows.astype(F32) + jnp.dot(rows, polynomial, preferred_element_type=F32)
+        blocks = pl.ds(pl.multiple_of(group * 4, 4), 4)
+        result[blocks, 0:ROWS, :] = total[:, 0:128].astype(BF16).reshape(4, ROWS, 128)
+        tail = total[:, 128:192].reshape(4, ROWS, 64)
+        result[blocks, ROWS:72, :] = jnp.concatenate([tail[:, 0:24], tail[:, 24:48]], axis=2).astype(BF16)
 
         def send(i, carry):
-            b = rem(me + i, BLOCKS)
-            remote(result.at[b], back.at[chip], b_send, b_recv, block(b))
+            j = group * 4 + rem(i + y, 4)
+            b = 2 * j + core
+
+            @pl.when(b != me)
+            def _():
+                remote(result.at[j], back.at[chip], b_send, b_recv, block(b))
+
+            @pl.when(b == me)
+            def _():
+                pltpu.make_async_copy(result.at[j], back.at[chip], b_recv).start()
+
             return carry
 
-        lax.fori_loop(1, BLOCKS, send, 0)
-        back[chip] = result[me]
-
-    loads[1].wait()
-
-    @pl.when(core == 0)
-    def _():
-        wait(back.at[pl.ds(0, SLOTS_OWN - 1)], b_recv)
-
-    @pl.when(core == 1)
-    def _():
-        wait(back, b_recv)
-
-    for s in range(SLOTS_OWN):
-        kept, taken = keep[s : s + 1, :], step_size[s : s + 1, :]
-        fresh = back[s].astype(F32)
-        wgt[s, :, 0:128] = (wgt[s, :, 0:128] * kept - taken * fresh[0:ROWS]) * slot_root[s : s + 1, :]
-        tail = jnp.concatenate([fresh[ROWS:72, 0:64], fresh[ROWS:72, 64:128]], axis=0)
-        wgt[s, :, 128:192] = (wgt[s, :, 128:192] * kept - taken * tail) * slot_gamma[s : s + 1, :]
-
-    stores[1].start()
+        lax.fori_loop(0, 4, send, 0)
+        return carry
+
+    lax.fori_loop(0, 4, finish_group, 0)
+    wait(back, b_recv)
 
     for k in range(CHUNKS):
         for half in range(2):
@@ -410,30 +409,60 @@
         wait(outgoing.at[k, pl.ds(0, OWNERS - 1)], z_send.at[k])
     wait(peaks.at[pl.ds(0, 3)], l_send)
 
-    @pl.when(core == 0)
-    def _():
-        wait(send_a.at[pl.ds(0, SLOTS_OWN - 1)], x_send.at[0])
-        wait(send_b.at[pl.ds(0, SLOTS_OWN - 1)], x_send.at[1])
-        wait(result.at[pl.ds(0, BLOCKS - 1)], b_send)
-
-    @pl.when(core == 1)
-    def _():
-        wait(send_a, x_send.at[0])
-        wait(send_b, x_send.at[1])
-
+    wait(send_a.at[others], x_send.at[0])
+    wait(send_b.at[others], x_send.at[1])
+    wait(gram_mine, g_send)
+    wait(result.at[others], b_send)
     for copy in stores:
         copy.wait()
 
 
-def place(mom, wgt, kwt, momentum_out, weight_out, k_out, sem):
-    copies = [
-        pltpu.make_async_copy(mom, momentum_out, sem.at[0]),
-        pltpu.make_async_copy(wgt, weight_out, sem.at[1]),
-        pltpu.make_async_copy(kwt, k_out, sem.at[2]),
+def finish(
+    made_momentum, made_k, made_scales, made_rows, weight,
+    momentum_out, weight_out, k_out,
+    mom, kwt, scales, rows, wgt, in_sem, row_sem, weight_sem, out_sem, weight_out_sem,
+):
+    groups = [pl.ds(4 * g, 4) for g in range(4)]
+    scale_in = pltpu.make_async_copy(made_scales, scales, in_sem.at[0])
+    scale_in.start()
+    rows_in = [pltpu.make_async_copy(made_rows.at[g], rows.at[g], row_sem.at[i]) for i, g in enumerate(groups)]
+    weight_in = [pltpu.make_async_copy(weight.at[g], wgt.at[g], weight_sem.at[i]) for i, g in enumerate(groups)]
+    plain_in = [
+        pltpu.make_async_copy(made_momentum, mom, in_sem.at[1]),
+        pltpu.make_async_copy(made_k, kwt, in_sem.at[2]),
     ]
-    for copy in copies:
+    plain_out = [
+        pltpu.make_async_copy(mom, momentum_out, out_sem.at[0]),
+        pltpu.make_async_copy(kwt, k_out, out_sem.at[1]),
+    ]
+    weight_back = [
+        pltpu.make_async_copy(wgt.at[g], weight_out.at[g], weight_out_sem.at[i]) for i, g in enumerate(groups)
+    ]
+    for i in range(2):
+        rows_in[i].start()
+        weight_in[i].start()
+    for copy in plain_in:
         copy.start()
-    for copy in copies:
+    for i in range(2, 4):
+        rows_in[i].start()
+        weight_in[i].start()
+    scale_in.wait()
+    for i in range(4):
+        if i == 2:
+            for arriving, leaving in zip(plain_in, plain_out):
+                arriving.wait()
+                leaving.start()
+        rows_in[i].wait()
+        weight_in[i].wait()
+        for s in range(4 * i, 4 * i + 4):
+            kept, taken = scales[s : s + 1, 0:1], scales[s : s + 1, 1:2]
+            root, gamma = scales[s : s + 1, 2:3], scales[s : s + 1, 3:4]
+            fresh = rows[s].astype(F32)
+            wgt[s, :, 0:128] = (wgt[s, :, 0:128] * kept - taken * fresh[0:ROWS]) * root
+            tail = jnp.concatenate([fresh[ROWS:72, 0:64], fresh[ROWS:72, 64:128]], axis=0)
+            wgt[s, :, 128:192] = (wgt[s, :, 128:192] * kept - taken * tail) * gamma
+        weight_back[i].start()
+    for copy in weight_back + plain_out:
         copy.wait()
 
 
@@ -443,20 +472,22 @@
     vmem = pl.BlockSpec(memory_space=pltpu.VMEM)
     dma = pltpu.SemaphoreType.DMA
     wide = (4, ROWS, 128)
-    outs = (
-        jax.ShapeDtypeStruct(momentum.shape, F32),
-        jax.ShapeDtypeStruct(q_weight.shape, F32),
-        jax.ShapeDtypeStruct(k_weight.shape, F32),
-    )
+    momentum_like = jax.ShapeDtypeStruct(momentum.shape, F32)
+    k_like = jax.ShapeDtypeStruct(k_weight.shape, F32)
     made = pl.pallas_call(
         kernel,
-        out_shape=outs,
-        in_specs=[hbm] * 6,
-        out_specs=(hbm,) * 3,
+        out_shape=(
+            momentum_like,
+            k_like,
+            jax.ShapeDtypeStruct((SLOTS_OWN, 128), F32),
+            jax.ShapeDtypeStruct((SLOTS_OWN, 72, 128), BF16),
+        ),
+        in_specs=[hbm] * 5,
+        out_specs=(hbm,) * 4,
         scratch_shapes=[
             pltpu.VMEM(momentum.shape, F32),
-            pltpu.VMEM(q_weight.shape, F32),
             pltpu.VMEM(k_weight.shape, F32),
+            pltpu.VMEM((SLOTS_OWN, 128), F32),
             pltpu.VMEM((CHUNKS, HEADS_OWN, WIDTH, QR), BF16),
             pltpu.VMEM((CHUNKS, 2, 4, 2, 2) + wide, BF16),
             pltpu.VMEM((CHUNKS, 2, 2, 2) + wide, BF16),
@@ -480,26 +511,39 @@
             pltpu.VMEM((4, 8, 128), F32),
             pltpu.VMEM((SLOTS_OWN, ROWS, 128), BF16),
             pltpu.VMEM((SLOTS_OWN, 24, 128), BF16),
-            pltpu.VMEM((BLOCKS, ROWS, 128), BF16),
-            pltpu.VMEM((BLOCKS, 24, 128), BF16),
-            pltpu.VMEM((BLOCKS, 72, 128), BF16),
+            pltpu.VMEM((SLOTS_OWN, ROWS, 128), BF16),
+            pltpu.VMEM((SLOTS_OWN, 24, 128), BF16),
+            pltpu.VMEM((QK, QK), F32),
+            pltpu.VMEM((QK, QK), F32),
+            pltpu.VMEM((QR // 2, QK), BF16),
             pltpu.VMEM((SLOTS_OWN, 72, 128), BF16),
             dma((CHUNKS,)),
-            dma((6,)),
+            dma((5,)),
         ]
         + [dma((CHUNKS, 2))] * 10
-        + [dma((CHUNKS,)), dma((CHUNKS,)), dma((2,)), dma((2,)), dma, dma, dma, dma, dma((3,))],
+        + [dma((CHUNKS,)), dma((CHUNKS,)), dma((2,)), dma((2,)), dma, dma, dma, dma, dma, dma, dma((3,))],
         compiler_params=pltpu.CompilerParams(
             collective_id=0, has_side_effects=True, vmem_limit_bytes=56 * 1024 * 1024
         ),
-    )(assignment.reshape(1, HEADS), turned, momentum, q_weight, k_weight, max_logits)
+    )(assignment.reshape(1, HEADS), turned, momentum, k_weight, max_logits)
     return pl.pallas_call(
-        place,
-        out_shape=outs,
-        in_specs=[vmem] * 3,
+        finish,
+        out_shape=(momentum_like, jax.ShapeDtypeStruct(q_weight.shape, F32), k_like),
+        in_specs=[hbm] * 5,
         out_specs=(hbm,) * 3,
-        scratch_shapes=[dma((3,))],
-    )(*made)
+        scratch_shapes=[
+            pltpu.VMEM(momentum.shape, F32),
+            pltpu.VMEM(k_weight.shape, F32),
+            pltpu.VMEM((SLOTS_OWN, 128), F32),
+            pltpu.VMEM((SLOTS_OWN, 72, 128), BF16),
+            pltpu.VMEM(q_weight.shape, F32),
+            dma((3,)),
+            dma((4,)),
+            dma((4,)),
+            dma((2,)),
+            dma((4,)),
+        ],
+    )(*made, q_weight)
 
 
 def solution(mesh):

time: 70.1 us -> 69.5 us (level)
  no operation moved by 1% of the time
where the time goes in v3:
time: 69.5 us; the launch traced here: 69.4 us
  Pallas kernels  68.7 us (99%)
    pallas_call x1, Pallas kernels, body(): pl.pallas_call(kernel, out_shape=(momentum_like, k_like, jax.ShapeDtypeSt...  66.1 us
    pallas_call x1, Pallas kernels, body(): pl.pallas_call(finish, out_shape=(momentum_like, jax.ShapeDtypeStruct(q_w...  2.6 us

profile of v3, /device:TPU:1, one launch (start us, length us, event | category | flops | bytes accessed | tf_op | source)
XLA Modules:
  0.0 69.4 jit_solution(13295717478157865309)
XLA Ops:
  0.6 66.1 %shard_map.85 = (f32[16,48,192]{2,1,0:T(8,128)}, f32[8,16,128]{2,1,0:T(8,128)}, f32[16,128]{1,0:T(8,128)}, bf16[16,72,128]{2,1,0:T(8,128)(2,1)}) custom-call(s32[1,64]{1,0:T(1,128)} %bitcast.5, bf16[8,192,1536]{2,1,0:T(8,128)(2,1)} %bitcast.4, f32[16,48,192]{2,1,0:T(8,128)} %momentum.1, f32[8,16,128]{2,1,0:T(8,128)} %k_weight.1, f32[1,64]{1,0:T(1,128)} %logits.1), custom_call_target="tpu_custom_call" | custom-call | tf_op jit(solution)/shard_map/pallas_call | solution.py:477
  66.8 2.6 %shard_map.86 = (f32[16,48,192]{2,1,0:T(8,128)}, f32[16,48,192]{2,1,0:T(8,128)}, f32[8,16,128]{2,1,0:T(8,128)}) custom-call(f32[16,48,192]{2,1,0:T(8,128)} %get-tuple-element.7.made_momentum, f32[8,16,128]{2,1,0:T(8,128)} %get-tuple-element.8.made_k, f32[16,128]{1,0:T(8,128)} %get-tuple-element.9.made_scales, ...), custom_call_target="tpu_custom_call" | custom-call | tf_op jit(solution)/shard_map/pallas_call | solution.py:529

commit v4 on v3

--- a/solution.py
+++ b/solution.py
@@ -98,14 +98,21 @@
     barrier = pltpu.get_barrier_semaphore()
 
     def greet(i, carry):
-        pl.semaphore_signal(barrier, inc=1, device_id=block(rem(me + i, BLOCKS)), device_id_type=MESH)
+        pl.semaphore_signal(barrier, inc=1, device_id=block(rem(me + 2 * i, BLOCKS)), device_id_type=MESH)
         return carry
 
     def greet_z(i, carry):
         pl.semaphore_signal(barrier, inc=1, device_id={"owner": rem(z + i, OWNERS)}, device_id_type=MESH)
         return carry
 
-    lax.fori_loop(1, BLOCKS, greet, 0)
+    lax.fori_loop(1, BLOCKS // 2, greet, 0)
+    beside = 1 - core
+    near = (
+        at(x, y, beside), at(rem(x + 1, 4), y, beside), at(rem(x + 3, 4), y, beside), at(rem(x + 2, 4), y, beside),
+        at(x, rem(y + 1, 4), beside), at(x, rem(y + 3, 4), beside),
+    )
+    for device in near:
+        pl.semaphore_signal(barrier, inc=1, device_id=device, device_id_type=MESH)
     lax.fori_loop(1, OWNERS, greet_z, 0)
 
     row_at = lax.broadcasted_iota(jnp.int32, (384, 384), 0)
@@ -244,7 +251,7 @@
         target[div(me, 2)] = source[chip]
 
     pack(0)
-    pl.semaphore_wait(barrier, BLOCKS - 1 + OWNERS - 1)
+    pl.semaphore_wait(barrier, BLOCKS // 2 - 1 + len(near) + OWNERS - 1)
     start_relays(0)
     pack(1)
     start_relays(1)

time: 69.5 us -> 68.5 us (0.986)
  Pallas kernels: 68.7 us -> 67.8 us
    pallas_call x1, Pallas kernels: 66.1 us -> 65.2 us  [body(): pl.pallas_call(kernel, out_shape=(momentum_like, k_like, jax.ShapeDtypeSt...]
where the time goes in v4:
time: 68.5 us; the launch traced here: 68.4 us
  Pallas kernels  67.8 us (99%)
    pallas_call x1, Pallas kernels, body(): pl.pallas_call(kernel, out_shape=(momentum_like, k_like, jax.ShapeDtypeSt...  65.2 us
    pallas_call x1, Pallas kernels, body(): pl.pallas_call(finish, out_shape=(momentum_like, jax.ShapeDtypeStruct(q_w...  2.6 us

profile of v4, /device:TPU:1, one launch (start us, length us, event | category | flops | bytes accessed | tf_op | source)
XLA Modules:
  0.0 68.4 jit_solution(17285673391075157087)
XLA Ops:
  0.6 65.2 %shard_map.85 = (f32[16,48,192]{2,1,0:T(8,128)}, f32[8,16,128]{2,1,0:T(8,128)}, f32[16,128]{1,0:T(8,128)}, bf16[16,72,128]{2,1,0:T(8,128)(2,1)}) custom-call(s32[1,64]{1,0:T(1,128)} %bitcast.5, bf16[8,192,1536]{2,1,0:T(8,128)(2,1)} %bitcast.4, f32[16,48,192]{2,1,0:T(8,128)} %momentum.1, f32[8,16,128]{2,1,0:T(8,128)} %k_weight.1, f32[1,64]{1,0:T(1,128)} %logits.1), custom_call_target="tpu_custom_call" | custom-call | tf_op jit(solution)/shard_map/pallas_call | solution.py:484
  65.8 2.6 %shard_map.86 = (f32[16,48,192]{2,1,0:T(8,128)}, f32[16,48,192]{2,1,0:T(8,128)}, f32[8,16,128]{2,1,0:T(8,128)}) custom-call(f32[16,48,192]{2,1,0:T(8,128)} %get-tuple-element.7.made_momentum, f32[8,16,128]{2,1,0:T(8,128)} %get-tuple-element.8.made_k, f32[16,128]{1,0:T(8,128)} %get-tuple-element.9.made_scales, ...), custom_call_target="tpu_custom_call" | custom-call | tf_op jit(solution)/shard_map/pallas_call | solution.py:536

commit v5 on v3

--- a/solution.py
+++ b/solution.py
@@ -40,7 +40,10 @@
 
 
 def dot_f32(a, b):
-    return jnp.dot(a, b, precision=lax.Precision.HIGHEST, preferred_element_type=F32)
+    a_high, b_high = a.astype(BF16), b.astype(BF16)
+    a_low, b_low = (a - a_high.astype(F32)).astype(BF16), (b - b_high.astype(F32)).astype(BF16)
+    dot = functools.partial(jnp.dot, preferred_element_type=F32)
+    return dot(a_high, b_high) + (dot(a_high, b_low) + dot(a_low, b_high))
 
 
 def kernel(
@@ -97,15 +100,16 @@
 
     barrier = pltpu.get_barrier_semaphore()
 
-    def greet(i, carry):
-        pl.semaphore_signal(barrier, inc=1, device_id=block(rem(me + i, BLOCKS)), device_id_type=MESH)
-        return carry
-
     def greet_z(i, carry):
         pl.semaphore_signal(barrier, inc=1, device_id={"owner": rem(z + i, OWNERS)}, device_id_type=MESH)
         return carry
 
-    lax.fori_loop(1, BLOCKS, greet, 0)
+    beside = 1 - core
+    near = [at(x, y, beside)]
+    for c in range(2):
+        near += [at(rem(x + i, 4), y, c) for i in (1, 2, 3)] + [at(x, rem(y + i, 4), c) for i in (1, 3)]
+    for device in near:
+        pl.semaphore_signal(barrier, inc=1, device_id=device, device_id_type=MESH)
     lax.fori_loop(1, OWNERS, greet_z, 0)
 
     row_at = lax.broadcasted_iota(jnp.int32, (384, 384), 0)
@@ -244,7 +248,7 @@
         target[div(me, 2)] = source[chip]
 
     pack(0)
-    pl.semaphore_wait(barrier, BLOCKS - 1 + OWNERS - 1)
+    pl.semaphore_wait(barrier, len(near) + OWNERS - 1)
     start_relays(0)
     pack(1)
     start_relays(1)

time: 69.5 us -> 67 us (0.964)
  Pallas kernels: 68.7 us -> 66.2 us
    pallas_call x1, Pallas kernels: 66.1 us -> 63.6 us  [body(): pl.pallas_call(kernel, out_shape=(momentum_like, k_like, jax.ShapeDtypeSt...]
where the time goes in v5:
time: 67 us; the launch traced here: 66.9 us
  Pallas kernels  66.2 us (99%)
    pallas_call x1, Pallas kernels, body(): pl.pallas_call(kernel, out_shape=(momentum_like, k_like, jax.ShapeDtypeSt...  63.6 us
    pallas_call x1, Pallas kernels, body(): pl.pallas_call(finish, out_shape=(momentum_like, jax.ShapeDtypeStruct(q_w...  2.6 us

profile of v5, /device:TPU:1, one launch (start us, length us, event | category | flops | bytes accessed | tf_op | source)
XLA Modules:
  0.0 66.9 jit_solution(5229870801520588732)
XLA Ops:
  0.6 63.6 %shard_map.85 = (f32[16,48,192]{2,1,0:T(8,128)}, f32[8,16,128]{2,1,0:T(8,128)}, f32[16,128]{1,0:T(8,128)}, bf16[16,72,128]{2,1,0:T(8,128)(2,1)}) custom-call(s32[1,64]{1,0:T(1,128)} %bitcast.5, bf16[8,192,1536]{2,1,0:T(8,128)(2,1)} %bitcast.4, f32[16,48,192]{2,1,0:T(8,128)} %momentum.1, f32[8,16,128]{2,1,0:T(8,128)} %k_weight.1, f32[1,64]{1,0:T(1,128)} %logits.1), custom_call_target="tpu_custom_call" | custom-call | tf_op jit(solution)/shard_map/pallas_call | solution.py:481
  64.3 2.6 %shard_map.86 = (f32[16,48,192]{2,1,0:T(8,128)}, f32[16,48,192]{2,1,0:T(8,128)}, f32[8,16,128]{2,1,0:T(8,128)}) custom-call(f32[16,48,192]{2,1,0:T(8,128)} %get-tuple-element.7.made_momentum, f32[8,16,128]{2,1,0:T(8,128)} %get-tuple-element.8.made_k, f32[16,128]{1,0:T(8,128)} %get-tuple-element.9.made_scales, ...), custom_call_target="tpu_custom_call" | custom-call | tf_op jit(solution)/shard_map/pallas_call | solution.py:533

commit v6 on v5

--- a/solution.py
+++ b/solution.py
@@ -399,7 +399,8 @@
 
             return carry
 
-        lax.fori_loop(0, 4, send, 0)
+        for i in range(4):
+            send(jnp.int32(i), 0)
         return carry
 
     lax.fori_loop(0, 4, finish_group, 0)

time: 67 us -> 67 us (level)
  no operation moved by 1% of the time
where the time goes in v6:
time: 67 us; the launch traced here: 66.9 us
  Pallas kernels  66.2 us (99%)
    pallas_call x1, Pallas kernels, body(): pl.pallas_call(kernel, out_shape=(momentum_like, k_like, jax.ShapeDtypeSt...  63.6 us
    pallas_call x1, Pallas kernels, body(): pl.pallas_call(finish, out_shape=(momentum_like, jax.ShapeDtypeStruct(q_w...  2.6 us

profile of v6, /device:TPU:1, one launch (start us, length us, event | category | flops | bytes accessed | tf_op | source)
XLA Modules:
  0.0 66.9 jit_solution(12266826350718737401)
XLA Ops:
  0.6 63.6 %shard_map.85 = (f32[16,48,192]{2,1,0:T(8,128)}, f32[8,16,128]{2,1,0:T(8,128)}, f32[16,128]{1,0:T(8,128)}, bf16[16,72,128]{2,1,0:T(8,128)(2,1)}) custom-call(s32[1,64]{1,0:T(1,128)} %bitcast.5, bf16[8,192,1536]{2,1,0:T(8,128)(2,1)} %bitcast.4, f32[16,48,192]{2,1,0:T(8,128)} %momentum.1, f32[8,16,128]{2,1,0:T(8,128)} %k_weight.1, f32[1,64]{1,0:T(1,128)} %logits.1), custom_call_target="tpu_custom_call" | custom-call | tf_op jit(solution)/shard_map/pallas_call | solution.py:482
  64.3 2.6 %shard_map.86 = (f32[16,48,192]{2,1,0:T(8,128)}, f32[16,48,192]{2,1,0:T(8,128)}, f32[8,16,128]{2,1,0:T(8,128)}) custom-call(f32[16,48,192]{2,1,0:T(8,128)} %get-tuple-element.7.made_momentum, f32[8,16,128]{2,1,0:T(8,128)} %get-tuple-element.8.made_k, f32[16,128]{1,0:T(8,128)} %get-tuple-element.9.made_scales, ...), custom_call_target="tpu_custom_call" | custom-call | tf_op jit(solution)/shard_map/pallas_call | solution.py:534
